TPU v7x, 32 devices: a whole 2x2x4 slice. The times are simulated.
32 devices in a mesh: rhombus: 4 (over z), tile: 8 (over y, x, core).
Axes of the slice: x: 2, y: 2, z: 4, core: 2. Of those that a mesh axis runs over, the one named last changes fastest.
Arguments:
- fine_latent: bfloat16 [16384, 512], P(('rhombus', 'tile')), may hold values from -6 to 6
- mid_latent: bfloat16 [1024, 512], P(('rhombus', 'tile')), may hold values from -6 to 6
- coarse_latent: bfloat16 [642, 512], replicated, may hold values from -6 to 6
- fine_parent: int32 [16384], P(('rhombus', 'tile')), may hold values from 0 to 95, as said below
- mid_parent: int32 [1024], P(('rhombus', 'tile')), may hold values from 0 to 641
- halo_rows: int32 [8192], P(('rhombus', 'tile')), may hold values from 0 to 511
- edge_source: int32 [98304], P(('rhombus', 'tile')), may hold values from 0 to 767
- edge_target: int32 [98304], P(('rhombus', 'tile')), may hold values from 0 to 512, as said below
- w_child: bfloat16 [512, 512], replicated, may hold values from -1 to 1
- mid_w1: bfloat16 [512, 512], replicated, may hold values from -0.25 to 0.25
- mid_w2: bfloat16 [512, 512], replicated, may hold values from -0.5 to 0.5
- mid_w3: bfloat16 [512, 512], replicated, may hold values from -0.25 to 0.25
- w_coarse: bfloat16 [512, 512], replicated, may hold values from -1 to 1
- coarse_w1: bfloat16 [512, 512], replicated, may hold values from -0.25 to 0.25
- coarse_w2: bfloat16 [512, 512], replicated, may hold values from -0.5 to 0.5
- coarse_w3: bfloat16 [512, 512], replicated, may hold values from -0.25 to 0.25
- w_descend: bfloat16 [512, 512], replicated, may hold values from -0.25 to 0.25
- w_fine: bfloat16 [512, 512], replicated, may hold values from -0.25 to 0.25
- edge_w_src: bfloat16 [512, 512], replicated, may hold values from -1 to 1
- edge_w_dst: bfloat16 [512, 512], replicated, may hold values from -0.25 to 0.25
- edge_w2: bfloat16 [512, 512], replicated, may hold values from -0.25 to 0.25
- node_w1: bfloat16 [512, 512], replicated, may hold values from -0.25 to 0.25
- node_w2: bfloat16 [512, 512], replicated, may hold values from -0.125 to 0.125
- node_w3: bfloat16 [512, 512], replicated, may hold values from -0.25 to 0.25
Outputs:
- fine_out: bfloat16 [16384, 512], P(('rhombus', 'tile'))
- mid_out: bfloat16 [1024, 512], P(('rhombus', 'tile'))
- coarse_out: bfloat16 [642, 512], replicated
Inputs may be any that keep to these rules, and one draw needn't show every extreme that they name: `fine_parent`: in tile t of a group, an entry p < 32 names a middle slot of the same tile, 32 <= p < 64 a slot of tile t - 1, 64 <= p a slot of tile t + 1; tile 0 never names the tile before and the last tile of a group never names the tile after. `edge_target`: in each tile the live slots come first and name a fine row of that tile; the remaining slots hold 512. Each tile has at least 1536 live slots, and some tile has all 3072 slots live.
All inputs are finite; a program needn't handle non-finite values.
Results may differ from a plain program's by a relative error of at most 0.013.
Values may be sent and summed in bfloat16 or wider, within the bound.
A program may use at most 64 MiB of HBM per device.

v0:
```python
import jax
import jax.numpy as jnp
from jax import lax
from jax.experimental import pallas as pl
from jax.experimental.pallas import tpu as pltpu
from jax.sharding import PartitionSpec as P

MESH = pl.DeviceIdType.MESH

EPSILON = 1e-05


def product(left, right):
    return jnp.dot(left, right, preferred_element_type=jnp.float32)


def normed(values):
    return values / jnp.sqrt(jnp.mean(values * values, axis=-1, keepdims=True) + EPSILON)


def gate(values):
    return values * (0.5 + 0.5 * jnp.tanh(0.5 * values))


def one_hot(ids, axis, shape):
    return jnp.where(lax.broadcasted_iota(jnp.int32, shape, axis) == ids, 1.0, 0.0).astype(jnp.bfloat16)


def as_columns(row, width):
    count = row.shape[1]
    column = jnp.transpose(jnp.broadcast_to(row, (128, count)))
    return jnp.concatenate([column] * (width // 128), axis=1)


def sweep_kernel(
    groups,
    tiles,
    parent_ref,
    halo_ref,
    latent_ref,
    coarse_id_ref,
    source_ref,
    target_ref,
    coarse_ref,
    fine_ref,
    *rest_refs,
):
    weight_refs = rest_refs[:16]
    fine_out_ref, mid_out_ref, coarse_out_ref = rest_refs[16:19]
    ups_ref, ids_ref, rim_ref, rim_parent_ref, fine_v, weights_v = rest_refs[19:25]
    sums_v, beside_v, picked_v, picked_parent_v, kept_v, flip_v, into_v = rest_refs[25:32]
    coarse_v, down_v, table_v, sent_v, got_v, edge_v = rest_refs[32:38]
    load_sem, near_send, near_recv, tree_send, block_recv, id_recv = rest_refs[38:]
    group, tile = (lax.axis_index("rhombus"), lax.axis_index("tile"))
    pairs = tiles // 2
    pair, core = (tile // 2, tile % 2)
    mids = latent_ref.shape[0]
    rims = halo_ref.shape[1] // 2
    fines, features = fine_ref.shape

    bf16, f32 = (jnp.bfloat16, jnp.float32)
    loads = [pltpu.make_async_copy(fine_ref, fine_v, load_sem.at[len(weight_refs)])]
    loads += [pltpu.make_async_copy(ref, weights_v.at[i], load_sem.at[i]) for i, ref in enumerate(weight_refs)]
    for load in loads:
        load.start()

    def weight(i):
        loads[i + 1].wait()
        return weights_v[i]

    def at(group_id, pair_id, core_id):
        return (group_id, pair_id * 2 + core_id)

    columns = [at((group + k) % groups, pair, core) for k in range(1, groups)]
    if pairs == 4:
        across, along = (pair + 1 - 2 * (pair % 2), (pair + 2) % 4)
        corner = (across + 2) % 4
        level = [across, along]
    else:
        level = [(pair + k) % pairs for k in range(1, pairs)]
    row_peers = [at(group, other, core) for other in level]
    partner = at(group, pair, 1 - core)
    peers = columns + row_peers + [partner]

    barrier = pltpu.get_barrier_semaphore()
    for peer in peers:
        pl.semaphore_signal(barrier, inc=1, device_id=peer, device_id_type=MESH)

    @pl.when(tile > 0)
    def _():
        pl.semaphore_signal(barrier, inc=1, device_id=(group, tile - 1), device_id_type=MESH)

    @pl.when(tile < tiles - 1)
    def _():
        pl.semaphore_signal(barrier, inc=1, device_id=(group, tile + 1), device_id_type=MESH)

    me = group * tiles + tile
    halves = groups * pairs

    def place_of(group_id, pair_id, core_id):
        return core_id * halves + group_id * pairs + pair_id

    mine = place_of(group, pair, core)
    ids_ref[mine] = coarse_id_ref[...]
    loads[0].wait()
    fine = fine_v[...]
    parents = parent_ref[...]
    picker = one_hot(parents, 0, (3 * mids, fines))
    sums_v[...] = product(picker, fine)
    pl.semaphore_wait(barrier, len(peers) + 1 + (tile + tiles - 1) // tiles - (tile + 1) // tiles)

    def near(index, source, target, device):
        return pltpu.make_async_remote_copy(
            src_ref=source,
            dst_ref=target,
            send_sem=near_send.at[index],
            recv_sem=near_recv.at[index],
            device_id=device,
            device_id_type=MESH,
        )

    before, after = ((group, tile - 1), (group, tile + 1))
    to_before = [
        near(0, sums_v.at[pl.ds(mids, mids)], beside_v.at[0], before),
        near(1, picked_v.at[pl.ds(0, rims)], rim_ref.at[pl.ds(rims, rims)], before),
        near(2, picked_parent_v.at[0], rim_parent_ref.at[1], before),
    ]
    to_after = [
        near(3, sums_v.at[pl.ds(2 * mids, mids)], beside_v.at[1], after),
        near(4, picked_v.at[pl.ds(rims, rims)], rim_ref.at[pl.ds(0, rims)], after),
        near(5, picked_parent_v.at[1], rim_parent_ref.at[0], after),
    ]

    @pl.when(tile > 0)
    def _():
        to_before[0].start()

    @pl.when(tile < tiles - 1)
    def _():
        to_after[0].start()

    halo = halo_ref[...]
    picked_v[...] = product(one_hot(as_columns(halo, fines), 1, (2 * rims, fines)), fine).astype(jnp.bfloat16)
    side = parents // mids
    shift = jnp.where(side == 1, -1, jnp.where(side == 2, 1, 0))
    global_parents = (me + shift) * mids + parents % mids
    parent_column = jnp.transpose(jnp.broadcast_to(global_parents, (128, fines)))
    for half in range(2):
        hit = lax.broadcasted_iota(jnp.int32, (fines, rims), 0) == halo[:, half * rims : (half + 1) * rims]
        spread = jnp.concatenate([parent_column] * (rims // 128), axis=1)
        picked_parent_v[half] = jnp.sum(jnp.where(hit, spread, 0), axis=0, keepdims=True)

    @pl.when(tile > 0)
    def _():
        to_before[1].start()
        to_before[2].start()

    @pl.when(tile < tiles - 1)
    def _():
        to_after[1].start()
        to_after[2].start()

    child_w = weight(0)
    kept = product(latent_ref[...], weight(1))

    @pl.when(tile > 0)
    def _():
        to_after[0].wait_recv()

    @pl.when(tile == 0)
    def _():
        beside_v[1] = jnp.zeros_like(beside_v[1])
        rim_ref[pl.ds(0, rims)] = jnp.zeros((rims, rim_ref.shape[1]), rim_ref.dtype)
        rim_parent_ref[0] = jnp.full(rim_parent_ref.shape[1:], -1, jnp.int32)

    @pl.when(tile < tiles - 1)
    def _():
        to_before[0].wait_recv()

    @pl.when(tile == tiles - 1)
    def _():
        beside_v[0] = jnp.zeros_like(beside_v[0])
        rim_ref[pl.ds(rims, rims)] = jnp.zeros((rims, rim_ref.shape[1]), rim_ref.dtype)
        rim_parent_ref[1] = jnp.full(rim_parent_ref.shape[1:], -1, jnp.int32)

    total = sums_v[pl.ds(0, mids)] + beside_v[0] + beside_v[1]
    leading = total.astype(jnp.bfloat16)
    rest = (total - leading.astype(jnp.float32)).astype(jnp.bfloat16)
    mid_in = (product(leading, child_w) + product(rest, child_w)).astype(jnp.bfloat16)
    hidden = gate(kept + product(mid_in, weight(2))).astype(jnp.bfloat16)
    mid_up = latent_ref[...].astype(jnp.float32) + normed(product(hidden, weight(3)))
    ups_ref[mine] = mid_up.astype(jnp.bfloat16)

    started = []

    def copies(slot, index, device):
        return [
            pltpu.make_async_remote_copy(
                src_ref=held.at[slot],
                dst_ref=held.at[slot],
                send_sem=tree_send.at[kind, index],
                recv_sem=sems.at[slot],
                device_id=device,
                device_id_type=MESH,
            )
            for kind, (held, sems) in enumerate([(ups_ref, block_recv), (ids_ref, id_recv)])
        ]

    def send(slot, devices):
        for device in devices:
            for copy in copies(slot, len(started) // 2, device):
                copy.start()
                started.append(copy)

    def arrive(slot):
        for copy in copies(slot, 0, partner):
            copy.wait_recv()

    def slot_of(k, pair_id, core_id):
        return place_of((group + k) % groups, pair_id, core_id)

    order = [0] + sorted(range(1, groups), key=lambda k: min(k, groups - k))
    send(mine, columns + row_peers + [partner])
    coarse = coarse_ref[...]
    kept_v[...] = product(coarse, weight(4))
    flip_v[0] = jnp.transpose(weight(5))
    flip_v[1] = jnp.transpose(weight(6))
    for k in order:
        if k > 0:
            slot = slot_of(k, pair, core)
            arrive(slot)
            send(slot, row_peers + [partner])
    for n, k in enumerate(order):
        for place, other in enumerate(level):
            slot = slot_of(k, other, core)
            arrive(slot)
            onward = [partner]
            if pairs == 4 and n % 2 == place:
                onward = [at(group, level[1 - place], core), partner]
            send(slot, onward)
    if pairs == 4:
        for k in order:
            slot = slot_of(k, corner, core)
            arrive(slot)
            send(slot, [partner])
    w_coarse = weight(7)
    coarse_count = coarse.shape[0]

    def half_sum(half):
        held = pl.ds(half * halves, halves)
        mid_msg = product(ups_ref[held].reshape(halves * mids, features), w_coarse).astype(bf16)
        id_row = jnp.concatenate([ids_ref[half * halves + d][:, :mids] for d in range(halves)], axis=1)
        return product(one_hot(id_row, 0, (coarse_count, halves * mids)), mid_msg)

    into_v[...] = half_sum(core)
    for k in order:
        for other in range(pairs):
            arrive(slot_of(k, other, 1 - core))

    @pl.when(tile > 0)
    def _():
        for copy in to_after[1:]:
            copy.wait_recv()

    @pl.when(tile < tiles - 1)
    def _():
        for copy in to_before[1:]:
            copy.wait_recv()

    coarse_in = (into_v[...] + half_sum(1 - core)).astype(bf16)
    hidden = gate(kept_v[...] + product(coarse_in, weight(8))).astype(bf16)
    updated = (coarse.astype(f32) + normed(product(hidden, weight(9)))).astype(bf16)
    coarse_out_ref[...] = updated
    padded = coarse_v.shape[0]
    edge = coarse_count // 16 * 16
    coarse_v[edge:] = jnp.zeros((padded - edge, features), bf16)
    coarse_v[:coarse_count] = updated

    nearby = []
    for d in range(-2, 3):
        other = (me + d + 2 * groups * tiles) % (groups * tiles)
        other_tile = other % tiles
        nearby.append(place_of(other // tiles, other_tile // 2, other_tile % 2))
    window = len(nearby) * mids
    spare = down_v.shape[0] - window
    near_row = jnp.concatenate(
        [ids_ref[slot][:, :mids] for slot in nearby] + [jnp.zeros((1, spare), jnp.int32)], axis=1
    )
    pick = one_hot(as_columns(near_row, padded)[:window], 1, (window, padded))
    picked = product(pick, coarse_v[...]).astype(bf16)
    down = product(picked, weight(10)).astype(bf16)
    near_up = jnp.concatenate([ups_ref[slot] for slot in nearby], axis=0)
    near_out = (near_up.astype(f32) + down.astype(f32)).astype(bf16)
    mid_out_ref[...] = near_out[2 * mids : 3 * mids]
    down_v[:window] = product(near_out, weight(11)).astype(bf16)
    down_v[window:] = jnp.zeros((spare, features), bf16)

    own_parent = (2 + shift) * mids + parents % mids
    far_parent = jnp.concatenate([rim_parent_ref[0], rim_parent_ref[1]], axis=1)
    far_parent = jnp.where(far_parent < 0, -1, far_parent - (me - 2) * mids)
    table_parent = jnp.concatenate([own_parent, far_parent], axis=1)
    width = down_v.shape[0]
    lift = one_hot(as_columns(table_parent, width), 1, (fines + 2 * rims, width))
    raised = product(lift, down_v[...])
    table_v[:fines] = (fine.astype(f32) + raised[:fines]).astype(bf16)
    table_v[fines:] = (rim_ref[...].astype(f32) + raised[fines:]).astype(bf16)

    across = (((1,), (1,)), ((), ()))

    def flipped(w, rows):
        return lax.dot_general(w, rows, across, preferred_element_type=f32).astype(bf16)

    lifted = table_v[:fines]
    sent_v[...] = flipped(flip_v[0], table_v[...])
    got_v[...] = flipped(flip_v[1], lifted)
    edge_v[...] = jnp.zeros(edge_v.shape, f32)
    edges = source_ref.shape[1]
    step = next(size for size in (1024, 512, 256, 128) if edges % size == 0)

    def block(i, carry):
        at = pl.ds(pl.multiple_of(i * step, step), step)
        source_pick = one_hot(source_ref[:, at], 0, (fines + 2 * rims, step))
        target_pick = one_hot(target_ref[:, at], 0, (fines, step))
        edge_sum = product(sent_v[...], source_pick) + product(got_v[...], target_pick)
        edge_hidden = gate(edge_sum).astype(bf16)
        edge_v[...] += lax.dot_general(target_pick, edge_hidden, across, preferred_element_type=f32)
        return carry

    lax.fori_loop(0, edges // step, block, 0)
    sums = edge_v[...]
    leading = sums.astype(bf16)
    rest = (sums - leading.astype(f32)).astype(bf16)
    e2 = weight(12)
    aggregate = (product(leading, e2) + product(rest, e2)).astype(bf16)
    hidden = gate(product(lifted, weight(13)) + product(aggregate, weight(14))).astype(bf16)
    fine_out_ref[...] = (lifted.astype(f32) + normed(product(hidden, weight(15)))).astype(bf16)

    @pl.when(tile > 0)
    def _():
        for copy in to_before:
            copy.wait_send()

    @pl.when(tile < tiles - 1)
    def _():
        for copy in to_after:
            copy.wait_send()

    for copy in started:
        copy.wait_send()


def on_device(
    fine_latent,
    mid_latent,
    coarse_latent,
    fine_parent,
    mid_parent,
    halo_rows,
    edge_source,
    edge_target,
    w_child,
    mid_w1,
    mid_w2,
    mid_w3,
    w_coarse,
    coarse_w1,
    coarse_w2,
    coarse_w3,
    w_descend,
    w_fine,
    edge_w_src,
    edge_w_dst,
    edge_w2,
    node_w1,
    node_w2,
    node_w3,
):
    groups, tiles = (lax.axis_size("rhombus"), lax.axis_size("tile"))
    devices = groups * tiles
    fines, features = fine_latent.shape
    mids = mid_latent.shape[0]
    halos = halo_rows.shape[0]
    rims = halos // 2
    coarse_count = coarse_latent.shape[0]
    weights = (
        w_child,
        mid_w1,
        mid_w2,
        mid_w3,
        coarse_w1,
        edge_w_src,
        edge_w_dst,
        w_coarse,
        coarse_w2,
        coarse_w3,
        w_descend,
        w_fine,
        edge_w2,
        node_w1,
        node_w2,
        node_w3,
    )
    ceil = lambda n: -(-n // 128) * 128
    width = ceil(mids)
    coarse_ids = jnp.pad(mid_parent[None, :], ((0, 0), (0, width - mids)))
    pairs = tiles // 2
    level = 2 if pairs == 4 else pairs - 1
    sends = groups + level + (groups - 1) * (level + 1) + groups * level
    sends += 2 * groups if pairs == 4 else 0
    bf16, f32, i32 = (jnp.bfloat16, jnp.float32, jnp.int32)
    vmem = pl.BlockSpec(memory_space=pltpu.VMEM)
    hbm = pl.BlockSpec(memory_space=pl.ANY)
    dma = pltpu.SemaphoreType.DMA
    return pl.pallas_call(
        lambda *refs: sweep_kernel(groups, tiles, *refs),
        out_shape=(
            jax.ShapeDtypeStruct((fines, features), bf16),
            jax.ShapeDtypeStruct((mids, features), bf16),
            jax.ShapeDtypeStruct((coarse_count, features), bf16),
        ),
        in_specs=[vmem] * 7 + [hbm] * (1 + len(weights)),
        out_specs=(vmem, vmem, vmem),
        scratch_shapes=[
            pltpu.VMEM((devices, mids, features), bf16),
            pltpu.VMEM((devices, 1, width), i32),
            pltpu.VMEM((halos, features), bf16),
            pltpu.VMEM((2, 1, rims), i32),
            pltpu.VMEM((fines, features), bf16),
            pltpu.VMEM((len(weights), features, features), bf16),
            pltpu.VMEM((3 * mids, features), f32),
            pltpu.VMEM((2, mids, features), f32),
            pltpu.VMEM((halos, features), bf16),
            pltpu.VMEM((2, 1, rims), i32),
            pltpu.VMEM((coarse_count, features), f32),
            pltpu.VMEM((2, features, features), bf16),
            pltpu.VMEM((coarse_count, features), f32),
            pltpu.VMEM((ceil(coarse_count), features), bf16),
            pltpu.VMEM((ceil(5 * mids), features), bf16),
            pltpu.VMEM((fines + halos, features), bf16),
            pltpu.VMEM((features, fines + halos), bf16),
            pltpu.VMEM((features, fines), bf16),
            pltpu.VMEM((fines, features), f32),
            dma((len(weights) + 1,)),
            dma((6,)),
            dma((6,)),
            dma((2, sends)),
            dma((devices,)),
            dma((devices,)),
        ],
        compiler_params=pltpu.CompilerParams(collective_id=0, has_side_effects=True),
        name="sweep",
    )(
        fine_parent[None, :],
        halo_rows[None, :],
        mid_latent,
        coarse_ids,
        edge_source[None, :],
        edge_target[None, :],
        coarse_latent,
        fine_latent,
        *weights,
    )


def solution(mesh):
    placed = (
        P(("rhombus", "tile"), None),
        P(("rhombus", "tile"), None),
        P(),
        P(("rhombus", "tile")),
        P(("rhombus", "tile")),
        P(("rhombus", "tile")),
        P(("rhombus", "tile")),
        P(("rhombus", "tile")),
        P(),
        P(),
        P(),
        P(),
        P(),
        P(),
        P(),
        P(),
        P(),
        P(),
        P(),
        P(),
        P(),
        P(),
        P(),
        P(),
    )
    return jax.shard_map(
        on_device,
        mesh=mesh,
        in_specs=placed,
        out_specs=(P(("rhombus", "tile"), None), P(("rhombus", "tile"), None), P()),
        check_vma=False,
    )
```

profile of v0, /device:TPU:11, one launch (start us, length us, event | category | flops | bytes accessed | tf_op | source)
XLA Modules:
  0.0 43.0 jit_solution(1026441405738339458)
XLA Ops:
  0.6 0.0 copy-start.2
  0.6 0.6 %copy-done.2 = s32[32]{0:T(128)S(1)} copy-done((s32[32]{0:T(128)S(1)}, s32[32]{0:T(128)}, u32[]{:S(2)}) %copy-start.2) | copy-done | bytes 152
  1.3 0.5 %pad.4.refs_3_ = s32[1,128]{1,0:T(1,128)} pad(s32[1,32]{1,0:T(1,128)S(1)} %bitcast.9, s32[]{:T(128)} %constant.0.clone.1), padding=0_0x0_96 | pad | bytes 644 | tf_op jit(solution)/shard_map/jit(_pad)/pad | solution.py:405
  1.8 37.7 %sweep.1 = (bf16[512,512]{1,0:T(8,128)(2,1)}, bf16[32,512]{1,0:T(8,128)(2,1)}, bf16[642,512]{1,0:T(8,128)(2,1)}) custom-call(s32[1,512]{1,0:T(1,128)} %bitcast.7, s32[1,256]{1,0:T(1,128)} %bitcast.8, bf16[32,512]{1,0:T(8,128)(2,1)} %refs_2_.1, s32[1,128]{1,0:T(1,128)} %pad.4.refs_3_, s32[1,3072]{1,0:T(1,128)} %bitcast.5, s32[1,3072]{1,0:T(1,128)} %bitcast.6, ...), custom_call_target="tpu_custom_call" | custom-call | tf_op jit(solution)/shard_map/sweep/pallas_call | solution.py:414
  39.5 0.0 copy-start
  39.6 0.0 copy-start.1
  39.6 1.9 %copy.30 = bf16[512,512]{1,0:T(8,128)(2,1)} copy(bf16[512,512]{1,0:T(8,128)(2,1)} %get-tuple-element.6) | data formatting | bytes 1048576
  41.5 0.0 copy-done.1
  41.5 0.6 %copy.31 = bf16[32,512]{1,0:T(8,128)(2,1)} copy(bf16[32,512]{1,0:T(8,128)(2,1)S(1)} %copy-done.1) | data formatting | bytes 65536
  42.1 0.0 copy-done
  42.1 0.8 %copy.32 = bf16[642,512]{1,0:T(8,128)(2,1)} copy(bf16[642,512]{1,0:T(8,128)(2,1)S(1)} %copy-done) | data formatting | bytes 1314816
Async XLA Ops:
  0.6 0.7 %copy-start.2 = (s32[32]{0:T(128)S(1)}, s32[32]{0:T(128)}, u32[]{:S(2)}) copy-start(s32[32]{0:T(128)} %param.28) | copy-start | bytes 388
  39.5 2.6 %copy-start = (bf16[642,512]{1,0:T(8,128)(2,1)S(1)}, bf16[642,512]{1,0:T(8,128)(2,1)}, u32[]{:S(2)}) copy-start(bf16[642,512]{1,0:T(8,128)(2,1)} %get-tuple-element.8) | copy-start | bytes 1972228
  39.6 2.0 %copy-start.1 = (bf16[32,512]{1,0:T(8,128)(2,1)S(1)}, bf16[32,512]{1,0:T(8,128)(2,1)}, u32[]{:S(2)}) copy-start(bf16[32,512]{1,0:T(8,128)(2,1)} %get-tuple-element.7) | copy-start | bytes 98308
where the time goes:
time: 43.2 us; the launch traced here: 43 us
  Pallas kernels  37.7 us (87%)
  local copies, waits for them, and re-layouts  4.56 us (11%)
  between operations  0.66 us (2%)
    pallas_call x1, Pallas kernels, on_device(): pl.pallas_call(lambda *refs: sweep_kernel(groups, tiles, *refs), out_shap...  37.7 us
    unnamed x9, local copies, waits for them, and re-layouts  4.05 us

commit v1 on v0

v1 whole, which is shorter than its diff:
```python
import jax
import jax.numpy as jnp
from jax import lax
from jax.experimental import pallas as pl
from jax.experimental.pallas import tpu as pltpu
from jax.sharding import PartitionSpec as P

MESH = pl.DeviceIdType.MESH

EPSILON = 1e-05

bf16, f32, i32 = (jnp.bfloat16, jnp.float32, jnp.int32)

ACROSS = (((1,), (1,)), ((), ()))


def product(left, right):
    return jnp.dot(left, right, preferred_element_type=f32)


def flipped(left, right):
    return lax.dot_general(left, right, ACROSS, preferred_element_type=f32)


def normed(values):
    return values / jnp.sqrt(jnp.mean(values * values, axis=-1, keepdims=True) + EPSILON)


def gate(values):
    return values * (0.5 + 0.5 * jnp.tanh(0.5 * values))


def one_hot(ids, axis, shape):
    return jnp.where(lax.broadcasted_iota(i32, shape, axis) == ids, 1.0, 0.0).astype(bf16)


def as_columns(row, width):
    count = row.shape[1]
    column = jnp.transpose(jnp.broadcast_to(row, (128, count)))
    return jnp.concatenate([column] * (width // 128), axis=1)


def ceil(n, unit=128):
    return -(-n // unit) * unit


GATHER_WEIGHTS = (
    "w_child",
    "mid_w2",
    "mid_w1",
    "mid_w3",
    "w_coarse",
    "coarse_w2",
    "edge_w_dst",
    "edge_w_src",
    "coarse_w1",
    "edge_w2",
    "node_w2",
)
FINISH_WEIGHTS = ("node_w1", "coarse_w3", "w_descend", "w_fine", "node_w3")
SMALL = ("parent", "halo", "coarse_id", "latent", "source", "target")


def gather_kernel(groups, tiles, *refs):
    refs = iter(refs)

    def take(n):
        return [next(refs) for _ in range(n)]

    small_refs = dict(zip(SMALL, take(len(SMALL))))
    fine_ref, coarse_ref = take(2)
    weight_refs = dict(zip(GATHER_WEIGHTS + FINISH_WEIGHTS, take(len(GATHER_WEIGHTS + FINISH_WEIGHTS))))
    pre_v, known_v, lookup_v, target_v, first_v, fine_v, coarse_v = take(7)
    near_v, pick_v, lift_v, flip_v, ending_v, handed_v = take(6)
    ups_ref, ids_ref, rim_ref, rim_parent_ref, weights_v = take(5)
    small_v = dict(zip(SMALL, take(len(SMALL))))
    side_v, beside_v, picked_v, picked_parent_v, table_v = take(5)
    load_sem, near_send, near_recv, tree_send, block_recv, id_recv = take(6)

    group, tile = (lax.axis_index("rhombus"), lax.axis_index("tile"))
    pairs = tiles // 2
    pair, core = (tile // 2, tile % 2)
    mids = small_v["latent"].shape[0]
    rims = small_v["halo"].shape[1] // 2
    fines, features = fine_v.shape
    coarse_count = coarse_v.shape[0]
    edges = small_v["source"].shape[1]

    def at(group_id, pair_id, core_id):
        return (group_id, pair_id * 2 + core_id)

    columns = [at((group + k) % groups, pair, core) for k in range(1, groups)]
    if pairs == 4:
        level = [pair + 1 - 2 * (pair % 2), (pair + 2) % 4]
        corner = (level[0] + 2) % 4
    else:
        level = [(pair + k) % pairs for k in range(1, pairs)]
    row_peers = [at(group, other, core) for other in level]
    partner = at(group, pair, 1 - core)
    peers = columns + row_peers + [partner]

    barrier = pltpu.get_barrier_semaphore()
    for peer in peers:
        pl.semaphore_signal(barrier, inc=1, device_id=peer, device_id_type=MESH)

    @pl.when(tile > 0)
    def _():
        pl.semaphore_signal(barrier, inc=1, device_id=(group, tile - 1), device_id_type=MESH)

    @pl.when(tile < tiles - 1)
    def _():
        pl.semaphore_signal(barrier, inc=1, device_id=(group, tile + 1), device_id_type=MESH)

    loads = {}

    def load(name, source, held):
        loads[name] = pltpu.make_async_copy(source, held, load_sem.at[len(loads)])
        loads[name].start()

    load("parent", small_refs["parent"], small_v["parent"])
    load("fine", fine_ref, fine_v)
    for name in ("halo", "latent", "coarse_id"):
        load(name, small_refs[name], small_v[name])
    held = {name: weights_v.at[i] for i, name in enumerate(GATHER_WEIGHTS)}
    held.update({name: handed_v.at[i] for i, name in enumerate(FINISH_WEIGHTS)})
    for name in GATHER_WEIGHTS[:8]:
        load(name, weight_refs[name], held[name])
    for name in ("source", "target"):
        load(name, small_refs[name], small_v[name])
    load("coarse", coarse_ref, coarse_v)
    for name in GATHER_WEIGHTS[8:] + FINISH_WEIGHTS:
        load(name, weight_refs[name], held[name])

    def weight(name):
        loads[name].wait()
        return held[name][...]

    me = group * tiles + tile
    halves = groups * pairs

    def place_of(group_id, pair_id, core_id):
        return core_id * halves + group_id * pairs + pair_id

    mine = place_of(group, pair, core)
    loads["parent"].wait()
    parents = small_v["parent"][...]
    picker = one_hot(parents, 0, (3 * mids, fines))
    loads["fine"].wait()
    sums = product(picker, fine_v[...])
    side_v[0] = sums[mids : 2 * mids].astype(bf16)
    side_v[1] = sums[2 * mids :].astype(bf16)
    pl.semaphore_wait(barrier, len(peers) + 1 + (tile + tiles - 1) // tiles - (tile + 1) // tiles)

    def near(index, source, target, device):
        return pltpu.make_async_remote_copy(
            src_ref=source,
            dst_ref=target,
            send_sem=near_send.at[index],
            recv_sem=near_recv.at[index],
            device_id=device,
            device_id_type=MESH,
        )

    before, after = ((group, tile - 1), (group, tile + 1))
    to_before = [
        near(0, side_v.at[0], beside_v.at[0], before),
        near(1, picked_v.at[pl.ds(0, rims)], rim_ref.at[pl.ds(rims, rims)], before),
        near(2, picked_parent_v.at[0], rim_parent_ref.at[1], before),
    ]
    to_after = [
        near(3, side_v.at[1], beside_v.at[1], after),
        near(4, picked_v.at[pl.ds(rims, rims)], rim_ref.at[pl.ds(0, rims)], after),
        near(5, picked_parent_v.at[1], rim_parent_ref.at[0], after),
    ]

    @pl.when(tile > 0)
    def _():
        to_before[0].start()

    @pl.when(tile < tiles - 1)
    def _():
        to_after[0].start()

    loads["halo"].wait()
    halo = small_v["halo"][...]
    picked_v[...] = product(one_hot(as_columns(halo, fines), 1, (2 * rims, fines)), fine_v[...]).astype(bf16)
    side = parents // mids
    shift = jnp.where(side == 1, -1, jnp.where(side == 2, 1, 0))
    within = parents % mids
    parent_column = jnp.transpose(jnp.broadcast_to((me + shift) * mids + within, (128, fines)))
    for half in range(2):
        hit = lax.broadcasted_iota(i32, (fines, rims), 0) == halo[:, half * rims : (half + 1) * rims]
        spread = jnp.concatenate([parent_column] * (rims // 128), axis=1)
        picked_parent_v[half] = jnp.sum(jnp.where(hit, spread, 0), axis=0, keepdims=True)

    @pl.when(tile > 0)
    def _():
        to_before[1].start()
        to_before[2].start()

    @pl.when(tile < tiles - 1)
    def _():
        to_after[1].start()
        to_after[2].start()

    child_mid = product(weight("w_child"), weight("mid_w2")).astype(bf16)
    loads["latent"].wait()
    kept_mid = product(small_v["latent"][...], weight("mid_w1"))
    loads["coarse_id"].wait()
    spare_ids = jnp.zeros((1, ids_ref.shape[2] - mids), i32)
    ids_ref[mine] = jnp.concatenate([small_v["coarse_id"][...], spare_ids], axis=1)
    msg_coarse = product(weight("w_coarse"), weight("coarse_w2")).astype(bf16)
    flip_v[1] = jnp.transpose(weight("edge_w_dst"))
    table_v[:features, fines + 2 * rims :] = flipped(flip_v[1], fine_v[...]).astype(bf16)
    flip_v[0] = jnp.transpose(weight("edge_w_src"))
    table_v[:features, :fines] = flipped(flip_v[0], fine_v[...]).astype(bf16)
    mid_w3 = weight("mid_w3")

    @pl.when(tile > 0)
    def _():
        to_after[0].wait_recv()

    @pl.when(tile == 0)
    def _():
        beside_v[1] = jnp.zeros_like(beside_v[1])
        rim_ref[pl.ds(0, rims)] = jnp.zeros((rims, features), bf16)
        rim_parent_ref[0] = jnp.full(rim_parent_ref.shape[1:], -1, i32)

    @pl.when(tile < tiles - 1)
    def _():
        to_before[0].wait_recv()

    @pl.when(tile == tiles - 1)
    def _():
        beside_v[0] = jnp.zeros_like(beside_v[0])
        rim_ref[pl.ds(rims, rims)] = jnp.zeros((rims, features), bf16)
        rim_parent_ref[1] = jnp.full(rim_parent_ref.shape[1:], -1, i32)

    total = (sums[:mids] + beside_v[0].astype(f32) + beside_v[1].astype(f32)).astype(bf16)
    hidden = gate(kept_mid + product(total, child_mid)).astype(bf16)
    mid_up = small_v["latent"][...].astype(f32) + normed(product(hidden, mid_w3))
    ups_ref[mine] = mid_up.astype(bf16)

    started = []

    def copies(slot, index, device):
        return [
            pltpu.make_async_remote_copy(
                src_ref=held.at[slot],
                dst_ref=held.at[slot],
                send_sem=tree_send.at[kind, index],
                recv_sem=sems.at[slot],
                device_id=device,
                device_id_type=MESH,
            )
            for kind, (held, sems) in enumerate([(ups_ref, block_recv), (ids_ref, id_recv)])
        ]

    def send(slot, devices):
        for device in devices:
            for copy in copies(slot, len(started) // 2, device):
                copy.start()
                started.append(copy)

    def arrive(slot):
        for copy in copies(slot, 0, partner):
            copy.wait_recv()

    def slot_of(k, pair_id, core_id):
        return place_of((group + k) % groups, pair_id, core_id)

    order = [0] + sorted(range(1, groups), key=lambda k: min(k, groups - k))
    send(mine, columns + row_peers + [partner])

    def keep_coarse():
        loads["coarse"].wait()
        pre_v[...] = product(coarse_v[...], weight("coarse_w1"))

    def keep_ending():
        ending_v[...] = product(weight("edge_w2"), weight("node_w2")).astype(bf16)

    def keep_first():
        first_v[...] = product(fine_v[...], weight("node_w1"))

    own_near = (1 + shift) * mids + within

    def fill_table():
        @pl.when(tile > 0)
        def _():
            for copy in to_after[1:]:
                copy.wait_recv()

        @pl.when(tile < tiles - 1)
        def _():
            for copy in to_before[1:]:
                copy.wait_recv()

        table_v[:features, fines : fines + 2 * rims] = flipped(flip_v[0], rim_ref[...]).astype(bf16)
        far = jnp.concatenate([rim_parent_ref[0], rim_parent_ref[1]], axis=1)
        far = jnp.where(far < 0, -1, far - (me - 2) * mids)
        blank = jnp.zeros((1, fines), i32)
        source_parent = jnp.concatenate([own_near + mids, far, blank], axis=1)
        target_parent = jnp.concatenate([blank, jnp.zeros((1, 2 * rims), i32), own_near], axis=1)
        line = lax.broadcasted_iota(i32, (table_v.shape[0] - features, table_v.shape[1]), 0)
        named = jnp.where(line == 0, source_parent, jnp.where(line == 1, target_parent, 0))
        table_v[features:] = named.astype(f32).astype(bf16)
        lift_v[...] = one_hot(as_columns(own_near, lift_v.shape[1]), 1, lift_v.shape)

    step = next(size for size in (512, 256, 128) if edges % size == 0)

    def known(i):
        span = pl.ds(i * step, step)
        source_pick = one_hot(small_v["source"][:, span], 0, (fines + 2 * rims, step))
        target_pick = one_hot(small_v["target"][:, span], 0, (fines, step))
        target_v[:, span] = target_pick
        found = product(table_v[...], jnp.concatenate([source_pick, target_pick], axis=0))
        known_v[:, span] = found[:features].astype(bf16)
        source_near = found[features : features + 1].astype(i32)
        target_near = found[features + 1 : features + 2].astype(i32) + 5 * mids
        line = lax.broadcasted_iota(i32, (8 * mids, step), 0)
        lookup_v[:, span] = jnp.where((line == source_near) | (line == target_near), 1.0, 0.0).astype(bf16)

    def load_edges():
        loads["source"].wait()
        loads["target"].wait()

    work = [keep_coarse, keep_ending, keep_first, fill_table, load_edges]
    work += [lambda i=i: known(i) for i in range(edges // step)]

    def do(n):
        for _ in range(min(n, len(work))):
            work.pop(0)()

    def coarse_part(slots):
        blocks = jnp.concatenate([ups_ref[slot] for slot in slots], axis=0)
        id_row = jnp.concatenate([ids_ref[slot][:, :mids] for slot in slots], axis=1)
        told = product(blocks, msg_coarse).astype(bf16)
        pre_v[...] += product(one_hot(id_row, 0, (coarse_count, len(slots) * mids)), told)

    do(4)
    for k in order:
        if k > 0:
            slot = slot_of(k, pair, core)
            arrive(slot)
            send(slot, row_peers + [partner])
    if pairs == 4:
        for n, k in enumerate(order):
            do(2 if n == 0 else 1)
            for place, other in enumerate(level):
                slot = slot_of(k, other, core)
                arrive(slot)
                onward = [partner]
                if n % 2 == place:
                    onward = [at(group, level[1 - place], core), partner]
                send(slot, onward)
        do(1)
        for k in order:
            slot = slot_of(k, corner, core)
            arrive(slot)
            send(slot, [partner])
        do(len(work))
        for k in order:
            arrive(slot_of(k, pair, 1 - core))
        coarse_part([slot_of(k, pair, c) for c in (core, 1 - core) for k in order])
        coarse_part([slot_of(k, other, core) for other in level for k in order])
        for other in level:
            for k in order:
                arrive(slot_of(k, other, 1 - core))
        coarse_part([slot_of(k, other, 1 - core) for other in level for k in order])
        for k in order:
            arrive(slot_of(k, corner, 1 - core))
        coarse_part([slot_of(k, corner, c) for c in (core, 1 - core) for k in order])
    else:
        for k in order:
            for other in level:
                slot = slot_of(k, other, core)
                arrive(slot)
                send(slot, [partner])
        do(len(work))
        for k in order:
            for other in range(pairs):
                arrive(slot_of(k, other, 1 - core))
        batch = next(size for size in (8, 4, 2, 1) if 2 * halves % size == 0)

        def part(i, carry):
            coarse_part([i * batch + j for j in range(batch)])
            return carry

        lax.fori_loop(0, 2 * halves // batch, part, 0)

    nearby = []
    for d in range(-2, 3):
        other = (me + d + 2 * groups * tiles) % (groups * tiles)
        other_tile = other % tiles
        nearby.append(place_of(other // tiles, other_tile // 2, other_tile % 2))
    window, padded = pick_v.shape
    spare = ceil(window) - window
    near_row = jnp.concatenate([ids_ref[slot][:, :mids] for slot in nearby] + [jnp.zeros((1, spare), i32)], axis=1)
    pick_v[...] = one_hot(as_columns(near_row, padded)[:window], 1, (window, padded))
    near_v[...] = jnp.concatenate([ups_ref[slot] for slot in nearby], axis=0)

    @pl.when(tile > 0)
    def _():
        for copy in to_before:
            copy.wait_send()

    @pl.when(tile < tiles - 1)
    def _():
        for copy in to_after:
            copy.wait_send()

    for copy in started:
        copy.wait_send()
    for name in FINISH_WEIGHTS[1:]:
        loads[name].wait()


def finish_kernel(*refs):
    pre_v, known_v, lookup_v, target_v, first_v, fine_v, coarse_v = refs[:7]
    near_v, pick_v, lift_v, flip_v, ending_v, handed_v = refs[7:13]
    fine_out_ref, mid_out_ref, coarse_out_ref = refs[13:16]
    fine_out_v, mid_out_v, coarse_out_v, padded_v, sums_v, out_sem = refs[16:]
    window, padded = pick_v.shape
    mids = mid_out_v.shape[0]
    fines, features = fine_v.shape
    coarse_count = coarse_v.shape[0]
    edges = known_v.shape[1]
    weights = {name: handed_v.at[i] for i, name in enumerate(FINISH_WEIGHTS)}
    outs = []

    def put(source, target):
        outs.append(pltpu.make_async_copy(source, target, out_sem.at[len(outs)]))
        outs[-1].start()

    hidden = gate(pre_v[...]).astype(bf16)
    updated = (coarse_v[...].astype(f32) + normed(product(hidden, weights["coarse_w3"][...]))).astype(bf16)
    coarse_out_v[...] = updated
    put(coarse_out_v, coarse_out_ref)
    edge = coarse_count // 16 * 16
    padded_v[edge:] = jnp.zeros((padded - edge, features), bf16)
    padded_v[:coarse_count] = updated

    picked = product(pick_v[...], padded_v[...]).astype(bf16)
    down = product(picked, weights["w_descend"][...])
    near_out = (near_v[...].astype(f32) + down).astype(bf16)
    mid_out_v[...] = near_out[2 * mids : 3 * mids]
    put(mid_out_v, mid_out_ref)
    fine_down = product(near_out, weights["w_fine"][...]).astype(bf16)
    beside = fine_down[mids : 4 * mids]

    def blank(rows):
        return jnp.zeros((rows, features), bf16)

    source_rows = jnp.concatenate([fine_down, blank(3 * mids)], axis=0)
    target_rows = jnp.concatenate([blank(5 * mids), beside], axis=0)
    change = (flipped(flip_v[0], source_rows) + flipped(flip_v[1], target_rows)).astype(bf16)

    step = next(size for size in (1024, 512, 256, 128) if edges % size == 0)
    total = None
    for i in range(edges // step):
        span = slice(i * step, (i + 1) * step)
        edge_sum = product(change, lookup_v[:, span]) + known_v[:, span].astype(f32)
        part = flipped(target_v[:, span], gate(edge_sum).astype(bf16))
        if i == 0:
            sums_v[...] = part
        else:
            sums_v[...] += part

    spare = lift_v.shape[1] - 3 * mids
    beside_first = product(beside, weights["node_w1"][...]).astype(bf16)
    lift = lift_v[...]
    if spare:
        beside = jnp.concatenate([beside, blank(spare)], axis=0)
        beside_first = jnp.concatenate([beside_first, blank(spare)], axis=0)
    lifted = (fine_v[...].astype(f32) + product(lift, beside)).astype(bf16)
    incoming = first_v[...] + product(lift, beside_first)
    incoming += product(sums_v[...].astype(bf16), ending_v[...])
    hidden = gate(incoming).astype(bf16)
    rows = fines // 2
    for half in range(2):
        span = slice(half * rows, (half + 1) * rows)
        result = lifted[span].astype(f32) + normed(product(hidden[span], weights["node_w3"][...]))
        fine_out_v[span] = result.astype(bf16)
        put(fine_out_v.at[span], fine_out_ref.at[span])
    for copy in outs:
        copy.wait()


def on_device(
    fine_latent,
    mid_latent,
    coarse_latent,
    fine_parent,
    mid_parent,
    halo_rows,
    edge_source,
    edge_target,
    w_child,
    mid_w1,
    mid_w2,
    mid_w3,
    w_coarse,
    coarse_w1,
    coarse_w2,
    coarse_w3,
    w_descend,
    w_fine,
    edge_w_src,
    edge_w_dst,
    edge_w2,
    node_w1,
    node_w2,
    node_w3,
):
    named = dict(
        w_child=w_child,
        mid_w1=mid_w1,
        mid_w2=mid_w2,
        mid_w3=mid_w3,
        w_coarse=w_coarse,
        coarse_w1=coarse_w1,
        coarse_w2=coarse_w2,
        coarse_w3=coarse_w3,
        w_descend=w_descend,
        w_fine=w_fine,
        edge_w_src=edge_w_src,
        edge_w_dst=edge_w_dst,
        edge_w2=edge_w2,
        node_w1=node_w1,
        node_w2=node_w2,
        node_w3=node_w3,
    )
    groups, tiles = (lax.axis_size("rhombus"), lax.axis_size("tile"))
    devices = groups * tiles
    fines, features = fine_latent.shape
    mids = mid_latent.shape[0]
    halos = halo_rows.shape[0]
    rims = halos // 2
    edges = edge_source.shape[0]
    coarse_count = coarse_latent.shape[0]
    width = ceil(mids)
    pairs = tiles // 2
    level = 2 if pairs == 4 else pairs - 1
    sends = groups + level + (groups - 1) * (level + 1) + groups * level
    sends += 2 * groups if pairs == 4 else 0
    vmem = pl.BlockSpec(memory_space=pltpu.VMEM)
    hbm = pl.BlockSpec(memory_space=pl.ANY)
    dma = pltpu.SemaphoreType.DMA
    square = (features, features)
    small = [fine_parent[None, :], halo_rows[None, :], mid_parent[None, :], mid_latent]
    small += [edge_source[None, :], edge_target[None, :]]
    weights = [named[name] for name in GATHER_WEIGHTS + FINISH_WEIGHTS]
    handed = (
        pltpu.VMEM((coarse_count, features), f32),
        pltpu.VMEM((features, edges), bf16),
        pltpu.VMEM((8 * mids, edges), bf16),
        pltpu.VMEM((fines, edges), bf16),
        pltpu.VMEM((fines, features), f32),
        pltpu.VMEM((fines, features), bf16),
        pltpu.VMEM((coarse_count, features), bf16),
        pltpu.VMEM((5 * mids, features), bf16),
        pltpu.VMEM((5 * mids, ceil(coarse_count)), bf16),
        pltpu.VMEM((fines, ceil(3 * mids)), bf16),
        pltpu.VMEM((2, *square), bf16),
        pltpu.VMEM(square, bf16),
        pltpu.VMEM((len(FINISH_WEIGHTS), *square), bf16),
    )
    between = pl.pallas_call(
        lambda *refs: gather_kernel(groups, tiles, *refs),
        out_shape=handed,
        in_specs=[hbm] * (len(small) + 2 + len(weights)),
        out_specs=(vmem,) * len(handed),
        scratch_shapes=[
            pltpu.VMEM((devices, mids, features), bf16),
            pltpu.VMEM((devices, 1, width), i32),
            pltpu.VMEM((halos, features), bf16),
            pltpu.VMEM((2, 1, rims), i32),
            pltpu.VMEM((len(GATHER_WEIGHTS), *square), bf16),
            *[pltpu.VMEM(array.shape, array.dtype) for array in small],
            pltpu.VMEM((2, mids, features), bf16),
            pltpu.VMEM((2, mids, features), bf16),
            pltpu.VMEM((halos, features), bf16),
            pltpu.VMEM((2, 1, rims), i32),
            pltpu.VMEM((features + 16, 2 * fines + halos), bf16),
            dma((len(small) + 2 + len(weights),)),
            dma((6,)),
            dma((6,)),
            dma((2, sends)),
            dma((devices,)),
            dma((devices,)),
        ],
        compiler_params=pltpu.CompilerParams(collective_id=0, has_side_effects=True, vmem_limit_bytes=40 << 20),
        name="sweep_gather",
    )(*small, fine_latent, coarse_latent, *weights)
    return pl.pallas_call(
        finish_kernel,
        out_shape=(
            jax.ShapeDtypeStruct((fines, features), bf16),
            jax.ShapeDtypeStruct((mids, features), bf16),
            jax.ShapeDtypeStruct((coarse_count, features), bf16),
        ),
        in_specs=[vmem] * len(handed),
        out_specs=(hbm,) * 3,
        scratch_shapes=[
            pltpu.VMEM((fines, features), bf16),
            pltpu.VMEM((mids, features), bf16),
            pltpu.VMEM((coarse_count, features), bf16),
            pltpu.VMEM((ceil(coarse_count), features), bf16),
            pltpu.VMEM((fines, features), f32),
            dma((4,)),
        ],
        compiler_params=pltpu.CompilerParams(vmem_limit_bytes=24 << 20),
        name="sweep_finish",
    )(*between)


def solution(mesh):
    split, rows, whole = (P(("rhombus", "tile")), P(("rhombus", "tile"), None), P())
    placed = (rows, rows, whole) + (split,) * 5 + (whole,) * 16
    return jax.shard_map(
        on_device,
        mesh=mesh,
        in_specs=placed,
        out_specs=(rows, rows, whole),
        check_vma=False,
    )
```

time: 43.2 us -> 33 us (0.76)
  the two profiles are of different devices: /device:TPU:11 before, /device:TPU:0 now
where the time goes in v1:
time: 33 us; the launch traced here: 32.8 us
  Pallas kernels  32.1 us (97%)
  between operations  0.65 us (2%)
    pallas_call x1, Pallas kernels, on_device(): pl.pallas_call(lambda *refs: gather_kernel(groups, tiles, *refs), out_sha...  25.3 us
    pallas_call x1, Pallas kernels, on_device(): pl.pallas_call(finish_kernel, out_shape=(jax.ShapeDtypeStruct((fines, fea...  6.87 us

profile of v1, /device:TPU:0, one launch (start us, length us, event | category | flops | bytes accessed | tf_op | source)
XLA Modules:
  0.0 32.8 jit_solution(6326654181035265960)
XLA Ops:
  0.6 25.3 %sweep_gather.1 = (f32[642,512]{1,0:T(8,128)S(1)}, bf16[512,3072]{1,0:T(8,128)(2,1)S(1)}, bf16[256,3072]{1,0:T(8,128)(2,1)S(1)}, bf16[512,3072]{1,0:T(8,128)(2,1...) custom-call(s32[1,512]{1,0:T(1,128)} %bitcast.7, ...), custom_call_target="tpu_custom_call" | custom-call | tf_op jit(solution)/shard_map/sweep_gather/pallas_call | solution.py:568
  25.9 6.9 %sweep_finish.1 = (bf16[512,512]{1,0:T(8,128)(2,1)}, bf16[32,512]{1,0:T(8,128)(2,1)}, bf16[642,512]{1,0:T(8,128)(2,1)}) custom-call(f32[642,512]{1,0:T(8,128)S(1)} %get-tuple-element.16.refs_0_, bf16[512,3072]{1,0:T(8,128)(2,1)S(1)} %get-tuple-element.17.refs_1_, bf16[256,3072]{1,0:T(8,128)(2,1)S(1)} %get-tuple-element.18.refs_2_, ...), custom_call_target="tpu_custom_call" | custom-call | tf_op jit(solution)/shard_map/sweep_finish/pallas_call | solution.py:595

commit v2 on v1

--- a/solution.py
+++ b/solution.py
@@ -49,16 +49,17 @@
     "mid_w2",
     "mid_w1",
     "mid_w3",
+    "edge_w_dst",
+    "edge_w_src",
     "w_coarse",
     "coarse_w2",
-    "edge_w_dst",
-    "edge_w_src",
     "coarse_w1",
     "edge_w2",
     "node_w2",
 )
 FINISH_WEIGHTS = ("node_w1", "coarse_w3", "w_descend", "w_fine", "node_w3")
-SMALL = ("parent", "halo", "coarse_id", "latent", "source", "target")
+SMALL = ("parent", "halo", "coarse_id", "latent")
+LOADS = (2, 2, 1, 1, 2, 1, 2)
 
 
 def gather_kernel(groups, tiles, *refs):
@@ -67,15 +68,16 @@
     def take(n):
         return [next(refs) for _ in range(n)]
 
-    small_refs = dict(zip(SMALL, take(len(SMALL))))
+    small_refs = dict(zip(SMALL + ("source", "target"), take(len(SMALL) + 2)))
     fine_ref, coarse_ref = take(2)
     weight_refs = dict(zip(GATHER_WEIGHTS + FINISH_WEIGHTS, take(len(GATHER_WEIGHTS + FINISH_WEIGHTS))))
     pre_v, known_v, lookup_v, target_v, first_v, fine_v, coarse_v = take(7)
     near_v, pick_v, lift_v, flip_v, ending_v, handed_v = take(6)
     ups_ref, ids_ref, rim_ref, rim_parent_ref, weights_v = take(5)
     small_v = dict(zip(SMALL, take(len(SMALL))))
-    side_v, beside_v, picked_v, picked_parent_v, table_v = take(5)
-    load_sem, near_send, near_recv, tree_send, block_recv, id_recv = take(6)
+    (edge_ids_v,) = take(1)
+    side_v, beside_v, picked_v, picked_parent_v, table_v, message_v, gained_v = take(7)
+    load_sem, near_send, near_recv, tree_send, block_recv, id_send, id_recv = take(7)
 
     group, tile = (lax.axis_index("rhombus"), lax.axis_index("tile"))
     pairs = tiles // 2
@@ -84,12 +86,16 @@
     rims = small_v["halo"].shape[1] // 2
     fines, features = fine_v.shape
     coarse_count = coarse_v.shape[0]
-    edges = small_v["source"].shape[1]
+    edges = edge_ids_v.shape[2]
 
     def at(group_id, pair_id, core_id):
         return (group_id, pair_id * 2 + core_id)
 
-    columns = [at((group + k) % groups, pair, core) for k in range(1, groups)]
+    if groups == 4:
+        heights = [group, group + 1 - 2 * (group % 2), (group + 2) % 4, 3 - group]
+    else:
+        heights = [(group + k) % groups for k in [0] + sorted(range(1, groups), key=lambda k: min(k, groups - k))]
+    columns = [at(height, pair, core) for height in heights[1:]]
     if pairs == 4:
         level = [pair + 1 - 2 * (pair % 2), (pair + 2) % 4]
         corner = (level[0] + 2) % 4
@@ -113,39 +119,58 @@
 
     loads = {}
 
-    def load(name, source, held):
-        loads[name] = pltpu.make_async_copy(source, held, load_sem.at[len(loads)])
-        loads[name].start()
-
-    load("parent", small_refs["parent"], small_v["parent"])
-    load("fine", fine_ref, fine_v)
+    def load(name, *pairs_of_refs, whole=None):
+        sem = load_sem.at[len(loads)]
+        for source, held in pairs_of_refs:
+            pltpu.make_async_copy(source, held, sem).start()
+        held = pairs_of_refs[0][1] if whole is None else whole
+        loads[name] = pltpu.make_async_copy(held, held, sem)
+
+    load("parent", (small_refs["parent"], small_v["parent"]))
+    load("fine", (fine_ref, fine_v))
     for name in ("halo", "latent", "coarse_id"):
-        load(name, small_refs[name], small_v[name])
+        load(name, (small_refs[name], small_v[name]))
     held = {name: weights_v.at[i] for i, name in enumerate(GATHER_WEIGHTS)}
     held.update({name: handed_v.at[i] for i, name in enumerate(FINISH_WEIGHTS)})
-    for name in GATHER_WEIGHTS[:8]:
-        load(name, weight_refs[name], held[name])
-    for name in ("source", "target"):
-        load(name, small_refs[name], small_v[name])
-    load("coarse", coarse_ref, coarse_v)
-    for name in GATHER_WEIGHTS[8:] + FINISH_WEIGHTS:
-        load(name, weight_refs[name], held[name])
+    first = 0
+    for n, count in enumerate(LOADS):
+        names = GATHER_WEIGHTS[first : first + count]
+        load(n, *[(weight_refs[name], held[name]) for name in names], whole=weights_v.at[pl.ds(first, count)])
+        first += count
+        if n == 1:
+            ids = [(small_refs[name], edge_ids_v.at[i]) for i, name in enumerate(("source", "target"))]
+            load("edges", *ids, whole=edge_ids_v)
+        if n == 4:
+            load("coarse", (coarse_ref, coarse_v))
+    load("node_w1", (weight_refs["node_w1"], held["node_w1"]))
+    rest = FINISH_WEIGHTS[1:]
+    load("handed", *[(weight_refs[name], held[name]) for name in rest], whole=handed_v.at[pl.ds(1, len(rest))])
+    waited = set()
+
+    def await_load(name):
+        if name not in waited:
+            loads[name].wait()
+            waited.add(name)
 
     def weight(name):
-        loads[name].wait()
+        if name == "node_w1":
+            await_load(name)
+        else:
+            place = GATHER_WEIGHTS.index(name)
+            await_load(next(n for n in range(len(LOADS)) if place < sum(LOADS[: n + 1])))
         return held[name][...]
 
     me = group * tiles + tile
     halves = groups * pairs
 
     def place_of(group_id, pair_id, core_id):
-        return core_id * halves + group_id * pairs + pair_id
+        return core_id * halves + pair_id * groups + group_id
 
     mine = place_of(group, pair, core)
-    loads["parent"].wait()
+    await_load("parent")
     parents = small_v["parent"][...]
     picker = one_hot(parents, 0, (3 * mids, fines))
-    loads["fine"].wait()
+    await_load("fine")
     sums = product(picker, fine_v[...])
     side_v[0] = sums[mids : 2 * mids].astype(bf16)
     side_v[1] = sums[2 * mids :].astype(bf16)
@@ -181,7 +206,53 @@
     def _():
         to_after[0].start()
 
-    loads["halo"].wait()
+    ids_sent = []
+
+    def pass_ids(first_slot, count, device, kind):
+        copy = pltpu.make_async_remote_copy(
+            src_ref=ids_ref.at[pl.ds(first_slot, count)],
+            dst_ref=ids_ref.at[pl.ds(first_slot, count)],
+            send_sem=id_send.at[0],
+            recv_sem=id_recv.at[kind],
+            device_id=device,
+            device_id_type=MESH,
+        )
+        copy.start()
+        ids_sent.append(count)
+
+    def await_ids(first_slot, count, kind):
+        held_ids = ids_ref.at[pl.ds(first_slot, count)]
+        pltpu.make_async_copy(held_ids, held_ids, id_recv.at[kind]).wait()
+
+    def column_of(pair_id, core_id):
+        return place_of(0, pair_id, core_id)
+
+    await_load("coarse_id")
+    spare_ids = jnp.zeros((1, ids_ref.shape[2] - mids), i32)
+    ids_ref[mine] = jnp.concatenate([small_v["coarse_id"][...], spare_ids], axis=1)
+    for device in columns:
+        pass_ids(mine, 1, device, 0)
+
+    def ids_across():
+        await_ids(0, groups - 1, 0)
+        for n, device in enumerate(row_peers):
+            pass_ids(column_of(pair, core), groups, device, 1 + n)
+
+    def ids_corner():
+        for n, other in enumerate(level):
+            await_ids(column_of(other, core), groups, 1 + n if pairs == 4 else len(level) - n)
+        if pairs == 4:
+            pass_ids(column_of(level[0], core), groups, row_peers[1], len(level) + 1)
+
+    def ids_partner():
+        if pairs == 4:
+            await_ids(column_of(corner, core), groups, len(level) + 1)
+        pass_ids(core * halves, halves, partner, len(level) + 2)
+
+    def ids_done():
+        await_ids((1 - core) * halves, halves, len(level) + 2)
+
+    await_load("halo")
     halo = small_v["halo"][...]
     picked_v[...] = product(one_hot(as_columns(halo, fines), 1, (2 * rims, fines)), fine_v[...]).astype(bf16)
     side = parents // mids
@@ -204,12 +275,8 @@
         to_after[2].start()
 
     child_mid = product(weight("w_child"), weight("mid_w2")).astype(bf16)
-    loads["latent"].wait()
+    await_load("latent")
     kept_mid = product(small_v["latent"][...], weight("mid_w1"))
-    loads["coarse_id"].wait()
-    spare_ids = jnp.zeros((1, ids_ref.shape[2] - mids), i32)
-    ids_ref[mine] = jnp.concatenate([small_v["coarse_id"][...], spare_ids], axis=1)
-    msg_coarse = product(weight("w_coarse"), weight("coarse_w2")).astype(bf16)
     flip_v[1] = jnp.transpose(weight("edge_w_dst"))
     table_v[:features, fines + 2 * rims :] = flipped(flip_v[1], fine_v[...]).astype(bf16)
     flip_v[0] = jnp.transpose(weight("edge_w_src"))
@@ -242,39 +309,42 @@
     ups_ref[mine] = mid_up.astype(bf16)
 
     started = []
-
-    def copies(slot, index, device):
-        return [
-            pltpu.make_async_remote_copy(
-                src_ref=held.at[slot],
-                dst_ref=held.at[slot],
-                send_sem=tree_send.at[kind, index],
-                recv_sem=sems.at[slot],
-                device_id=device,
-                device_id_type=MESH,
-            )
-            for kind, (held, sems) in enumerate([(ups_ref, block_recv), (ids_ref, id_recv)])
-        ]
-
-    def send(slot, devices):
+    sides = {"column": 0, "near": 1, "far": 2, "corner": 3}
+
+    def block_copy(slot, recv, device):
+        return pltpu.make_async_remote_copy(
+            src_ref=ups_ref.at[slot],
+            dst_ref=ups_ref.at[slot],
+            send_sem=tree_send.at[0],
+            recv_sem=block_recv.at[recv],
+            device_id=device,
+            device_id_type=MESH,
+        )
+
+    def send(pair_id, height, devices, side):
+        slot = place_of(height, pair_id, core)
         for device in devices:
-            for copy in copies(slot, len(started) // 2, device):
-                copy.start()
-                started.append(copy)
-
-    def arrive(slot):
-        for copy in copies(slot, 0, partner):
-            copy.wait_recv()
-
-    def slot_of(k, pair_id, core_id):
-        return place_of((group + k) % groups, pair_id, core_id)
-
-    order = [0] + sorted(range(1, groups), key=lambda k: min(k, groups - k))
-    send(mine, columns + row_peers + [partner])
+            own_way = device is not partner
+            copy = block_copy(slot, slot - core * halves if own_way else halves + side, device)
+            copy.start()
+            started.append(copy)
+
+    def arrive(pair_id, height):
+        slot = place_of(height, pair_id, core)
+        block_copy(slot, slot - core * halves, partner).wait_recv()
+
+    def arrive_column(pair_id, side):
+        held_blocks = ups_ref.at[pl.ds(column_of(pair_id, 1 - core), groups)]
+        pltpu.make_async_copy(held_blocks, held_blocks, block_recv.at[halves + side]).wait()
+
+    send(pair, group, columns[:1] + row_peers + columns[1:] + [partner], 0)
 
     def keep_coarse():
-        loads["coarse"].wait()
+        await_load("coarse")
         pre_v[...] = product(coarse_v[...], weight("coarse_w1"))
+
+    def keep_message():
+        message_v[...] = product(weight("w_coarse"), weight("coarse_w2")).astype(bf16)
 
     def keep_ending():
         ending_v[...] = product(weight("edge_w2"), weight("node_w2")).astype(bf16)
@@ -310,8 +380,8 @@
 
     def known(i):
         span = pl.ds(i * step, step)
-        source_pick = one_hot(small_v["source"][:, span], 0, (fines + 2 * rims, step))
-        target_pick = one_hot(small_v["target"][:, span], 0, (fines, step))
+        source_pick = one_hot(edge_ids_v[0, :, span], 0, (fines + 2 * rims, step))
+        target_pick = one_hot(edge_ids_v[1, :, span], 0, (fines, step))
         target_v[:, span] = target_pick
         found = product(table_v[...], jnp.concatenate([source_pick, target_pick], axis=0))
         known_v[:, span] = found[:features].astype(bf16)
@@ -320,83 +390,113 @@
         line = lax.broadcasted_iota(i32, (8 * mids, step), 0)
         lookup_v[:, span] = jnp.where((line == source_near) | (line == target_near), 1.0, 0.0).astype(bf16)
 
-    def load_edges():
-        loads["source"].wait()
-        loads["target"].wait()
-
-    work = [keep_coarse, keep_ending, keep_first, fill_table, load_edges]
-    work += [lambda i=i: known(i) for i in range(edges // step)]
-
-    def do(n):
-        for _ in range(min(n, len(work))):
-            work.pop(0)()
-
-    def coarse_part(slots):
-        blocks = jnp.concatenate([ups_ref[slot] for slot in slots], axis=0)
+    blocks_of_edges = iter(range(edges // step))
+
+    def do_known(n=1):
+        await_load("edges")
+        for i in [i for _, i in zip(range(n), blocks_of_edges)]:
+            known(i)
+
+    def coarse_part(places, rows_of):
+        blocks = jnp.concatenate([rows_of(place) for place in places], axis=0)
+        slots = [place + h for place in places for h in range(groups)]
         id_row = jnp.concatenate([ids_ref[slot][:, :mids] for slot in slots], axis=1)
-        told = product(blocks, msg_coarse).astype(bf16)
-        pre_v[...] += product(one_hot(id_row, 0, (coarse_count, len(slots) * mids)), told)
-
-    do(4)
-    for k in order:
-        if k > 0:
-            slot = slot_of(k, pair, core)
-            arrive(slot)
-            send(slot, row_peers + [partner])
-    if pairs == 4:
-        for n, k in enumerate(order):
-            do(2 if n == 0 else 1)
-            for place, other in enumerate(level):
-                slot = slot_of(k, other, core)
-                arrive(slot)
-                onward = [partner]
-                if n % 2 == place:
-                    onward = [at(group, level[1 - place], core), partner]
-                send(slot, onward)
-        do(1)
-        for k in order:
-            slot = slot_of(k, corner, core)
-            arrive(slot)
-            send(slot, [partner])
-        do(len(work))
-        for k in order:
-            arrive(slot_of(k, pair, 1 - core))
-        coarse_part([slot_of(k, pair, c) for c in (core, 1 - core) for k in order])
-        coarse_part([slot_of(k, other, core) for other in level for k in order])
-        for other in level:
-            for k in order:
-                arrive(slot_of(k, other, 1 - core))
-        coarse_part([slot_of(k, other, 1 - core) for other in level for k in order])
-        for k in order:
-            arrive(slot_of(k, corner, 1 - core))
-        coarse_part([slot_of(k, corner, c) for c in (core, 1 - core) for k in order])
-    else:
-        for k in order:
-            for other in level:
-                slot = slot_of(k, other, core)
-                arrive(slot)
-                send(slot, [partner])
-        do(len(work))
-        for k in order:
-            for other in range(pairs):
-                arrive(slot_of(k, other, 1 - core))
-        batch = next(size for size in (8, 4, 2, 1) if 2 * halves % size == 0)
-
-        def part(i, carry):
-            coarse_part([i * batch + j for j in range(batch)])
-            return carry
-
-        lax.fori_loop(0, 2 * halves // batch, part, 0)
+        return product(one_hot(id_row, 0, (coarse_count, len(slots) * mids)), blocks)
 
     nearby = []
     for d in range(-2, 3):
         other = (me + d + 2 * groups * tiles) % (groups * tiles)
         other_tile = other % tiles
         nearby.append(place_of(other // tiles, other_tile // 2, other_tile % 2))
-    window, padded = pick_v.shape
-    spare = ceil(window) - window
-    near_row = jnp.concatenate([ids_ref[slot][:, :mids] for slot in nearby] + [jnp.zeros((1, spare), i32)], axis=1)
-    pick_v[...] = one_hot(as_columns(near_row, padded)[:window], 1, (window, padded))
+
+    def find_near():
+        window, padded = pick_v.shape
+        spare = ceil(window) - window
+        near_row = jnp.concatenate([ids_ref[slot][:, :mids] for slot in nearby] + [jnp.zeros((1, spare), i32)], axis=1)
+        pick_v[...] = one_hot(as_columns(near_row, padded)[:window], 1, (window, padded))
+
+    def column_rows(place):
+        return ups_ref[pl.ds(place, groups)].reshape(groups * mids, features)
+
+    ids_across()
+    fill_table()
+    do_known()
+    if pairs == 4:
+        near_pair, far_pair = level
+
+        def across_at(n):
+            arrive(near_pair, heights[n])
+            send(near_pair, heights[n], ([row_peers[1]] if n % 2 == 0 else []) + [partner], 1)
+            arrive(far_pair, heights[n])
+            send(far_pair, heights[n], ([row_peers[0]] if n % 2 == 1 else []) + [partner], 2)
+
+        def corner_at(n):
+            arrive(corner, heights[n])
+            send(corner, heights[n], [partner], 3)
+
+        def column_at(n):
+            arrive(pair, heights[n])
+            send(pair, heights[n], row_peers + [partner], 0)
+
+        keep_message()
+        column_at(1)
+        across_at(0)
+        do_known()
+        ids_corner()
+        column_at(2)
+        keep_coarse()
+        column_at(3)
+        do_known()
+        across_at(1)
+        do_known()
+        ids_partner()
+        corner_at(0)
+        across_at(2)
+        keep_ending()
+        keep_first()
+        across_at(3)
+        corner_at(1)
+        do_known()
+        corner_at(2)
+        do_known(edges)
+        corner_at(3)
+        ids_done()
+        find_near()
+        mine_first = [column_of(p, core) for p in (pair, near_pair, far_pair, corner)]
+        arrive_column(pair, 0)
+        arrive_column(near_pair, 1)
+        arrive_column(far_pair, 2)
+        other_first = [column_of(p, 1 - core) for p in (pair, near_pair, far_pair)]
+        gained_v[...] = coarse_part(mine_first + other_first, column_rows)
+        arrive_column(corner, 3)
+        gained_v[...] += coarse_part([column_of(corner, 1 - core)], column_rows)
+    else:
+        for height in heights[1:]:
+            arrive(pair, height)
+            send(pair, height, row_peers + [partner], 0)
+        for height in heights:
+            for n, other in enumerate(level):
+                arrive(other, height)
+                send(other, height, [partner], 1 + n)
+        for keep in (keep_message, keep_coarse, keep_ending, keep_first):
+            keep()
+        do_known(edges)
+        ids_corner()
+        ids_partner()
+        ids_done()
+        for n, other in enumerate([pair] + level):
+            arrive_column(other, n)
+
+        find_near()
+        gained_v[...] = jnp.zeros_like(gained_v)
+
+        def part(i, carry):
+            gained_v[...] += coarse_part([i * groups], column_rows)
+            return carry
+
+        lax.fori_loop(0, 2 * pairs, part, 0)
+
+    pre_v[...] += product(gained_v[...].astype(bf16), message_v[...])
     near_v[...] = jnp.concatenate([ups_ref[slot] for slot in nearby], axis=0)
 
     @pl.when(tile > 0)
@@ -409,10 +509,14 @@
         for copy in to_after:
             copy.wait_send()
 
-    for copy in started:
-        copy.wait_send()
-    for name in FINISH_WEIGHTS[1:]:
-        loads[name].wait()
+    total = sum(ids_sent)
+    for first in range(0, total, ids_ref.shape[0]):
+        sent = ids_ref.at[pl.ds(0, min(total - first, ids_ref.shape[0]))]
+        pltpu.make_async_copy(sent, sent, id_send.at[0]).wait()
+    for first in range(0, len(started), ups_ref.shape[0]):
+        blocks = ups_ref.at[pl.ds(0, min(len(started) - first, ups_ref.shape[0]))]
+        pltpu.make_async_copy(blocks, blocks, tree_send.at[0]).wait()
+    await_load("handed")
 
 
 def finish_kernel(*refs):
@@ -541,14 +645,12 @@
     width = ceil(mids)
     pairs = tiles // 2
     level = 2 if pairs == 4 else pairs - 1
-    sends = groups + level + (groups - 1) * (level + 1) + groups * level
-    sends += 2 * groups if pairs == 4 else 0
     vmem = pl.BlockSpec(memory_space=pltpu.VMEM)
     hbm = pl.BlockSpec(memory_space=pl.ANY)
     dma = pltpu.SemaphoreType.DMA
     square = (features, features)
     small = [fine_parent[None, :], halo_rows[None, :], mid_parent[None, :], mid_latent]
-    small += [edge_source[None, :], edge_target[None, :]]
+    edge_ids = [edge_source[None, :], edge_target[None, :]]
     weights = [named[name] for name in GATHER_WEIGHTS + FINISH_WEIGHTS]
     handed = (
         pltpu.VMEM((coarse_count, features), f32),
@@ -568,7 +670,7 @@
     between = pl.pallas_call(
         lambda *refs: gather_kernel(groups, tiles, *refs),
         out_shape=handed,
-        in_specs=[hbm] * (len(small) + 2 + len(weights)),
+        in_specs=[hbm] * (len(small) + 4 + len(weights)),
         out_specs=(vmem,) * len(handed),
         scratch_shapes=[
             pltpu.VMEM((devices, mids, features), bf16),
@@ -577,21 +679,25 @@
             pltpu.VMEM((2, 1, rims), i32),
             pltpu.VMEM((len(GATHER_WEIGHTS), *square), bf16),
             *[pltpu.VMEM(array.shape, array.dtype) for array in small],
+            pltpu.VMEM((2, 1, edges), i32),
             pltpu.VMEM((2, mids, features), bf16),
             pltpu.VMEM((2, mids, features), bf16),
             pltpu.VMEM((halos, features), bf16),
             pltpu.VMEM((2, 1, rims), i32),
             pltpu.VMEM((features + 16, 2 * fines + halos), bf16),
-            dma((len(small) + 2 + len(weights),)),
+            pltpu.VMEM(square, bf16),
+            pltpu.VMEM((coarse_count, features), f32),
+            dma((len(small) + 5 + len(LOADS),)),
             dma((6,)),
             dma((6,)),
-            dma((2, sends)),
-            dma((devices,)),
-            dma((devices,)),
+            dma((1,)),
+            dma((groups * pairs + level + 2,)),
+            dma((1,)),
+            dma((level + 3,)),
         ],
         compiler_params=pltpu.CompilerParams(collective_id=0, has_side_effects=True, vmem_limit_bytes=40 << 20),
         name="sweep_gather",
-    )(*small, fine_latent, coarse_latent, *weights)
+    )(*small, *edge_ids, fine_latent, coarse_latent, *weights)
     return pl.pallas_call(
         finish_kernel,
         out_shape=(

time: 33 us -> 30.2 us (0.915)
  Pallas kernels: 32.1 us -> 29.4 us
    pallas_call x1, Pallas kernels: 25.3 us -> 22.5 us  [on_device(): pl.pallas_call(lambda *refs: gather_kernel(groups, tiles, *refs), out_sha...]
where the time goes in v2:
time: 30.2 us; the launch traced here: 30 us
  Pallas kernels  29.4 us (97%)
  between operations  0.65 us (2%)
    pallas_call x1, Pallas kernels, on_device(): pl.pallas_call(lambda *refs: gather_kernel(groups, tiles, *refs), out_sha...  22.5 us
    pallas_call x1, Pallas kernels, on_device(): pl.pallas_call(finish_kernel, out_shape=(jax.ShapeDtypeStruct((fines, fea...  6.87 us

profile of v2, /device:TPU:0, one launch (start us, length us, event | category | flops | bytes accessed | tf_op | source)
XLA Modules:
  0.0 30.0 jit_solution(12642992672682624341)
XLA Ops:
  0.6 22.5 %sweep_gather.1 = (f32[642,512]{1,0:T(8,128)S(1)}, bf16[512,3072]{1,0:T(8,128)(2,1)S(1)}, bf16[256,3072]{1,0:T(8,128)(2,1)S(1)}, bf16[512,3072]{1,0:T(8,128)(2,1...) custom-call(s32[1,512]{1,0:T(1,128)} %bitcast.7, ...), custom_call_target="tpu_custom_call" | custom-call | tf_op jit(solution)/shard_map/sweep_gather/pallas_call | solution.py:670
  23.1 6.9 %sweep_finish.1 = (bf16[512,512]{1,0:T(8,128)(2,1)}, bf16[32,512]{1,0:T(8,128)(2,1)}, bf16[642,512]{1,0:T(8,128)(2,1)}) custom-call(f32[642,512]{1,0:T(8,128)S(1)} %get-tuple-element.16.refs_0_, bf16[512,3072]{1,0:T(8,128)(2,1)S(1)} %get-tuple-element.17.refs_1_, bf16[256,3072]{1,0:T(8,128)(2,1)S(1)} %get-tuple-element.18.refs_2_, ...), custom_call_target="tpu_custom_call" | custom-call | tf_op jit(solution)/shard_map/sweep_finish/pallas_call | solution.py:701

commit v3 on v2

--- a/solution.py
+++ b/solution.py
@@ -72,11 +72,11 @@
     fine_ref, coarse_ref = take(2)
     weight_refs = dict(zip(GATHER_WEIGHTS + FINISH_WEIGHTS, take(len(GATHER_WEIGHTS + FINISH_WEIGHTS))))
     pre_v, known_v, lookup_v, target_v, first_v, fine_v, coarse_v = take(7)
-    near_v, pick_v, lift_v, flip_v, ending_v, handed_v = take(6)
+    near_v, pick_v, lift_v, flip_v, ending_v, handed_v, message_v, gained_v = take(8)
     ups_ref, ids_ref, rim_ref, rim_parent_ref, weights_v = take(5)
     small_v = dict(zip(SMALL, take(len(SMALL))))
     (edge_ids_v,) = take(1)
-    side_v, beside_v, picked_v, picked_parent_v, table_v, message_v, gained_v = take(7)
+    side_v, beside_v, picked_v, picked_parent_v, table_v = take(5)
     load_sem, near_send, near_recv, tree_send, block_recv, id_send, id_recv = take(7)
 
     group, tile = (lax.axis_index("rhombus"), lax.axis_index("tile"))
@@ -94,11 +94,12 @@
     if groups == 4:
         heights = [group, group + 1 - 2 * (group % 2), (group + 2) % 4, 3 - group]
     else:
-        heights = [(group + k) % groups for k in [0] + sorted(range(1, groups), key=lambda k: min(k, groups - k))]
+        order = [0] + sorted(range(1, groups), key=lambda k: min(k, groups - k))
+        heights = [(group + k) % groups for k in order]
     columns = [at(height, pair, core) for height in heights[1:]]
     if pairs == 4:
-        level = [pair + 1 - 2 * (pair % 2), (pair + 2) % 4]
-        corner = (level[0] + 2) % 4
+        beside = pair + 1 - 2 * (pair % 2)
+        level = [beside, (pair + 2) % 4, (beside + 2) % 4]
     else:
         level = [(pair + k) % pairs for k in range(1, pairs)]
     row_peers = [at(group, other, core) for other in level]
@@ -164,6 +165,9 @@
     halves = groups * pairs
 
     def place_of(group_id, pair_id, core_id):
+        return core_id * halves + group_id * pairs + pair_id
+
+    def id_place_of(group_id, pair_id, core_id):
         return core_id * halves + pair_id * groups + group_id
 
     mine = place_of(group, pair, core)
@@ -225,32 +229,27 @@
         pltpu.make_async_copy(held_ids, held_ids, id_recv.at[kind]).wait()
 
     def column_of(pair_id, core_id):
-        return place_of(0, pair_id, core_id)
+        return id_place_of(0, pair_id, core_id)
 
     await_load("coarse_id")
     spare_ids = jnp.zeros((1, ids_ref.shape[2] - mids), i32)
-    ids_ref[mine] = jnp.concatenate([small_v["coarse_id"][...], spare_ids], axis=1)
+    my_id = id_place_of(group, pair, core)
+    ids_ref[my_id] = jnp.concatenate([small_v["coarse_id"][...], spare_ids], axis=1)
     for device in columns:
-        pass_ids(mine, 1, device, 0)
+        pass_ids(my_id, 1, device, 0)
 
     def ids_across():
         await_ids(0, groups - 1, 0)
         for n, device in enumerate(row_peers):
             pass_ids(column_of(pair, core), groups, device, 1 + n)
 
-    def ids_corner():
+    def ids_partner():
         for n, other in enumerate(level):
             await_ids(column_of(other, core), groups, 1 + n if pairs == 4 else len(level) - n)
-        if pairs == 4:
-            pass_ids(column_of(level[0], core), groups, row_peers[1], len(level) + 1)
-
-    def ids_partner():
-        if pairs == 4:
-            await_ids(column_of(corner, core), groups, len(level) + 1)
-        pass_ids(core * halves, halves, partner, len(level) + 2)
+        pass_ids(core * halves, halves, partner, len(level) + 1)
 
     def ids_done():
-        await_ids((1 - core) * halves, halves, len(level) + 2)
+        await_ids((1 - core) * halves, halves, len(level) + 1)
 
     await_load("halo")
     halo = small_v["halo"][...]
@@ -309,35 +308,37 @@
     ups_ref[mine] = mid_up.astype(bf16)
 
     started = []
-    sides = {"column": 0, "near": 1, "far": 2, "corner": 3}
-
-    def block_copy(slot, recv, device):
-        return pltpu.make_async_remote_copy(
-            src_ref=ups_ref.at[slot],
-            dst_ref=ups_ref.at[slot],
-            send_sem=tree_send.at[0],
-            recv_sem=block_recv.at[recv],
-            device_id=device,
-            device_id_type=MESH,
-        )
-
-    def send(pair_id, height, devices, side):
-        slot = place_of(height, pair_id, core)
+
+    def send(pair_id, n, devices, recv):
+        slot = place_of(heights[n], pair_id, core)
         for device in devices:
-            own_way = device is not partner
-            copy = block_copy(slot, slot - core * halves if own_way else halves + side, device)
+            copy = pltpu.make_async_remote_copy(
+                src_ref=ups_ref.at[slot],
+                dst_ref=ups_ref.at[slot],
+                send_sem=tree_send.at[0],
+                recv_sem=block_recv.at[recv],
+                device_id=device,
+                device_id_type=MESH,
+            )
             copy.start()
             started.append(copy)
 
-    def arrive(pair_id, height):
-        slot = place_of(height, pair_id, core)
-        block_copy(slot, slot - core * halves, partner).wait_recv()
-
-    def arrive_column(pair_id, side):
-        held_blocks = ups_ref.at[pl.ds(column_of(pair_id, 1 - core), groups)]
-        pltpu.make_async_copy(held_blocks, held_blocks, block_recv.at[halves + side]).wait()
-
-    send(pair, group, columns[:1] + row_peers + columns[1:] + [partner], 0)
+    def arrive(first_slot, count, recv):
+        blocks = ups_ref.at[pl.ds(first_slot, count)]
+        pltpu.make_async_copy(blocks, blocks, block_recv.at[recv]).wait()
+
+    def place_in(n):
+        return n if groups == 4 else order.index((groups - order[n]) % groups)
+
+    def spread(n):
+        send(pair, n, row_peers, groups + n)
+        send(pair, n, [partner], 2 * groups + n)
+
+    for n in range(1, groups):
+        send(pair, 0, [columns[n - 1]], place_in(n))
+        if n == 1:
+            spread(0)
+
 
     def keep_coarse():
         await_load("coarse")
@@ -397,107 +398,78 @@
         for i in [i for _, i in zip(range(n), blocks_of_edges)]:
             known(i)
 
-    def coarse_part(places, rows_of):
-        blocks = jnp.concatenate([rows_of(place) for place in places], axis=0)
-        slots = [place + h for place in places for h in range(groups)]
+    def coarse_part(ns, cores):
+        places = [(heights[n], c) for c in cores for n in ns]
+        blocks = [ups_ref[pl.ds(place_of(h, 0, c), pairs)].reshape(pairs * mids, features) for h, c in places]
+        slots = [id_place_of(h, p, c) for h, c in places for p in range(pairs)]
         id_row = jnp.concatenate([ids_ref[slot][:, :mids] for slot in slots], axis=1)
-        return product(one_hot(id_row, 0, (coarse_count, len(slots) * mids)), blocks)
+        picker = one_hot(id_row, 0, (coarse_count, len(slots) * mids))
+        return product(picker, jnp.concatenate(blocks, axis=0))
 
     nearby = []
     for d in range(-2, 3):
         other = (me + d + 2 * groups * tiles) % (groups * tiles)
         other_tile = other % tiles
-        nearby.append(place_of(other // tiles, other_tile // 2, other_tile % 2))
+        nearby.append((other // tiles, other_tile // 2, other_tile % 2))
 
     def find_near():
         window, padded = pick_v.shape
         spare = ceil(window) - window
-        near_row = jnp.concatenate([ids_ref[slot][:, :mids] for slot in nearby] + [jnp.zeros((1, spare), i32)], axis=1)
+        near_row = jnp.concatenate([ids_ref[id_place_of(*place)][:, :mids] for place in nearby] + [jnp.zeros((1, spare), i32)], axis=1)
         pick_v[...] = one_hot(as_columns(near_row, padded)[:window], 1, (window, padded))
 
     def column_rows(place):
         return ups_ref[pl.ds(place, groups)].reshape(groups * mids, features)
 
+    def column_at(n):
+        arrive(place_of(heights[n], pair, core), 1, n)
+        spread(n)
+
+    def across_at(n):
+        arrive(0, len(level), groups + n)
+        for other in level:
+            send(other, n, [partner], 2 * groups + n)
+
+    def partner_at(n):
+        arrive(place_of(heights[n], 0, 1 - core), pairs, 2 * groups + n)
+
+    columns_left = iter(range(1, groups))
+    across_left = iter(range(groups))
+
+    def relay(left, step_at, n=1):
+        for i in [i for _, i in zip(range(n), left)]:
+            step_at(i)
+
+    keep_message()
     ids_across()
     fill_table()
     do_known()
-    if pairs == 4:
-        near_pair, far_pair = level
-
-        def across_at(n):
-            arrive(near_pair, heights[n])
-            send(near_pair, heights[n], ([row_peers[1]] if n % 2 == 0 else []) + [partner], 1)
-            arrive(far_pair, heights[n])
-            send(far_pair, heights[n], ([row_peers[0]] if n % 2 == 1 else []) + [partner], 2)
-
-        def corner_at(n):
-            arrive(corner, heights[n])
-            send(corner, heights[n], [partner], 3)
-
-        def column_at(n):
-            arrive(pair, heights[n])
-            send(pair, heights[n], row_peers + [partner], 0)
-
-        keep_message()
-        column_at(1)
-        across_at(0)
-        do_known()
-        ids_corner()
-        column_at(2)
-        keep_coarse()
-        column_at(3)
-        do_known()
-        across_at(1)
-        do_known()
-        ids_partner()
-        corner_at(0)
-        across_at(2)
-        keep_ending()
-        keep_first()
-        across_at(3)
-        corner_at(1)
-        do_known()
-        corner_at(2)
-        do_known(edges)
-        corner_at(3)
-        ids_done()
-        find_near()
-        mine_first = [column_of(p, core) for p in (pair, near_pair, far_pair, corner)]
-        arrive_column(pair, 0)
-        arrive_column(near_pair, 1)
-        arrive_column(far_pair, 2)
-        other_first = [column_of(p, 1 - core) for p in (pair, near_pair, far_pair)]
-        gained_v[...] = coarse_part(mine_first + other_first, column_rows)
-        arrive_column(corner, 3)
-        gained_v[...] += coarse_part([column_of(corner, 1 - core)], column_rows)
-    else:
-        for height in heights[1:]:
-            arrive(pair, height)
-            send(pair, height, row_peers + [partner], 0)
-        for height in heights:
-            for n, other in enumerate(level):
-                arrive(other, height)
-                send(other, height, [partner], 1 + n)
-        for keep in (keep_message, keep_coarse, keep_ending, keep_first):
-            keep()
-        do_known(edges)
-        ids_corner()
-        ids_partner()
-        ids_done()
-        for n, other in enumerate([pair] + level):
-            arrive_column(other, n)
-
-        find_near()
-        gained_v[...] = jnp.zeros_like(gained_v)
-
-        def part(i, carry):
-            gained_v[...] += coarse_part([i * groups], column_rows)
-            return carry
-
-        lax.fori_loop(0, 2 * pairs, part, 0)
-
-    pre_v[...] += product(gained_v[...].astype(bf16), message_v[...])
-    near_v[...] = jnp.concatenate([ups_ref[slot] for slot in nearby], axis=0)
+    relay(columns_left, column_at)
+    do_known()
+    relay(columns_left, column_at)
+    keep_coarse()
+    relay(columns_left, column_at, groups)
+    do_known()
+    relay(across_left, across_at)
+    ids_partner()
+    do_known()
+    keep_ending()
+    keep_first()
+    relay(across_left, across_at)
+    do_known()
+    relay(across_left, across_at)
+    ids_done()
+    find_near()
+    early = range(groups - 1)
+    gained_v[...] = coarse_part(early, [core])
+    relay(across_left, across_at, groups)
+    do_known(edges)
+    for n in early:
+        partner_at(n)
+    gained_v[...] += coarse_part(early, [1 - core])
+    partner_at(groups - 1)
+    gained_v[...] += coarse_part([groups - 1], [core, 1 - core])
+    near_v[...] = jnp.concatenate([ups_ref[place_of(*place)] for place in nearby], axis=0)
 
     @pl.when(tile > 0)
     def _():
@@ -521,9 +493,9 @@
 
 def finish_kernel(*refs):
     pre_v, known_v, lookup_v, target_v, first_v, fine_v, coarse_v = refs[:7]
-    near_v, pick_v, lift_v, flip_v, ending_v, handed_v = refs[7:13]
-    fine_out_ref, mid_out_ref, coarse_out_ref = refs[13:16]
-    fine_out_v, mid_out_v, coarse_out_v, padded_v, sums_v, out_sem = refs[16:]
+    near_v, pick_v, lift_v, flip_v, ending_v, handed_v, message_v, gained_v = refs[7:15]
+    fine_out_ref, mid_out_ref, coarse_out_ref = refs[15:18]
+    fine_out_v, mid_out_v, coarse_out_v, padded_v, sums_v, out_sem = refs[18:]
     window, padded = pick_v.shape
     mids = mid_out_v.shape[0]
     fines, features = fine_v.shape
@@ -536,7 +508,7 @@
         outs.append(pltpu.make_async_copy(source, target, out_sem.at[len(outs)]))
         outs[-1].start()
 
-    hidden = gate(pre_v[...]).astype(bf16)
+    hidden = gate(pre_v[...] + product(gained_v[...].astype(bf16), message_v[...])).astype(bf16)
     updated = (coarse_v[...].astype(f32) + normed(product(hidden, weights["coarse_w3"][...]))).astype(bf16)
     coarse_out_v[...] = updated
     put(coarse_out_v, coarse_out_ref)
@@ -644,7 +616,6 @@
     coarse_count = coarse_latent.shape[0]
     width = ceil(mids)
     pairs = tiles // 2
-    level = 2 if pairs == 4 else pairs - 1
     vmem = pl.BlockSpec(memory_space=pltpu.VMEM)
     hbm = pl.BlockSpec(memory_space=pl.ANY)
     dma = pltpu.SemaphoreType.DMA
@@ -666,6 +637,8 @@
         pltpu.VMEM((2, *square), bf16),
         pltpu.VMEM(square, bf16),
         pltpu.VMEM((len(FINISH_WEIGHTS), *square), bf16),
+        pltpu.VMEM(square, bf16),
+        pltpu.VMEM((coarse_count, features), f32),
     )
     between = pl.pallas_call(
         lambda *refs: gather_kernel(groups, tiles, *refs),
@@ -685,15 +658,13 @@
             pltpu.VMEM((halos, features), bf16),
             pltpu.VMEM((2, 1, rims), i32),
             pltpu.VMEM((features + 16, 2 * fines + halos), bf16),
-            pltpu.VMEM(square, bf16),
-            pltpu.VMEM((coarse_count, features), f32),
             dma((len(small) + 5 + len(LOADS),)),
             dma((6,)),
             dma((6,)),
             dma((1,)),
-            dma((groups * pairs + level + 2,)),
+            dma((3 * groups,)),
             dma((1,)),
-            dma((level + 3,)),
+            dma((pairs + 1,)),
         ],
         compiler_params=pltpu.CompilerParams(collective_id=0, has_side_effects=True, vmem_limit_bytes=40 << 20),
         name="sweep_gather",

time: 30.2 us -> 28.6 us (0.947)
  Pallas kernels: 29.4 us -> 27.8 us
    pallas_call x1, Pallas kernels: 22.5 us -> 20.5 us  [on_device(): pl.pallas_call(lambda *refs: gather_kernel(groups, tiles, *refs), out_sha...]
    pallas_call x1, Pallas kernels: 6.87 us -> 7.25 us  [on_device(): pl.pallas_call(finish_kernel, out_shape=(jax.ShapeDtypeStruct((fines, fea...]
where the time goes in v3:
time: 28.6 us; the launch traced here: 28.4 us
  Pallas kernels  27.8 us (97%)
  between operations  0.65 us (2%)
    pallas_call x1, Pallas kernels, on_device(): pl.pallas_call(lambda *refs: gather_kernel(groups, tiles, *refs), out_sha...  20.5 us
    pallas_call x1, Pallas kernels, on_device(): pl.pallas_call(finish_kernel, out_shape=(jax.ShapeDtypeStruct((fines, fea...  7.25 us

profile of v3, /device:TPU:0, one launch (start us, length us, event | category | flops | bytes accessed | tf_op | source)
XLA Modules:
  0.0 28.4 jit_solution(6720322341916548740)
XLA Ops:
  0.6 20.5 %sweep_gather.1 = (f32[642,512]{1,0:T(8,128)S(1)}, bf16[512,3072]{1,0:T(8,128)(2,1)S(1)}, bf16[256,3072]{1,0:T(8,128)(2,1)S(1)}, bf16[512,3072]{1,0:T(8,128)(2,1...) custom-call(s32[1,512]{1,0:T(1,128)} %bitcast.7, ...), custom_call_target="tpu_custom_call" | custom-call | tf_op jit(solution)/shard_map/sweep_gather/pallas_call | solution.py:643
  21.2 7.2 %sweep_finish.1 = (bf16[512,512]{1,0:T(8,128)(2,1)}, bf16[32,512]{1,0:T(8,128)(2,1)}, bf16[642,512]{1,0:T(8,128)(2,1)}) custom-call(f32[642,512]{1,0:T(8,128)S(1)} %get-tuple-element.18.refs_0_, bf16[512,3072]{1,0:T(8,128)(2,1)S(1)} %get-tuple-element.19.refs_1_, bf16[256,3072]{1,0:T(8,128)(2,1)S(1)} %get-tuple-element.20.refs_2_, ...), custom_call_target="tpu_custom_call" | custom-call | tf_op jit(solution)/shard_map/sweep_finish/pallas_call | solution.py:672

commit v4 on v3

--- a/solution.py
+++ b/solution.py
@@ -31,7 +31,8 @@
 
 
 def one_hot(ids, axis, shape):
-    return jnp.where(lax.broadcasted_iota(i32, shape, axis) == ids, 1.0, 0.0).astype(bf16)
+    line = lax.broadcasted_iota(jnp.int16, shape, axis)
+    return jnp.where(line == ids.astype(jnp.int16), jnp.ones((), bf16), jnp.zeros((), bf16))
 
 
 def as_columns(row, width):
@@ -54,12 +55,12 @@
     "w_coarse",
     "coarse_w2",
     "coarse_w1",
-    "edge_w2",
-    "node_w2",
 )
-FINISH_WEIGHTS = ("node_w1", "coarse_w3", "w_descend", "w_fine", "node_w3")
+FINISH_WEIGHTS = ("coarse_w3", "edge_w2", "node_w2", "w_descend", "w_fine", "node_w1", "node_w3")
+EARLY = 0
+BY_HEIGHT = (1, 2)
 SMALL = ("parent", "halo", "coarse_id", "latent")
-LOADS = (2, 2, 1, 1, 2, 1, 2)
+LOADS = (2, 2, 1, 1, 2, 1)
 
 
 def gather_kernel(groups, tiles, *refs):
@@ -71,12 +72,12 @@
     small_refs = dict(zip(SMALL + ("source", "target"), take(len(SMALL) + 2)))
     fine_ref, coarse_ref = take(2)
     weight_refs = dict(zip(GATHER_WEIGHTS + FINISH_WEIGHTS, take(len(GATHER_WEIGHTS + FINISH_WEIGHTS))))
-    pre_v, known_v, lookup_v, target_v, first_v, fine_v, coarse_v = take(7)
-    near_v, pick_v, lift_v, flip_v, ending_v, handed_v, message_v, gained_v = take(8)
+    pre_v, known_v, lookup_v, target_v, fine_v, coarse_v = take(6)
+    near_v, pick_v, lift_v, flip_v, handed_v, message_v, gained_v = take(7)
     ups_ref, ids_ref, rim_ref, rim_parent_ref, weights_v = take(5)
     small_v = dict(zip(SMALL, take(len(SMALL))))
     (edge_ids_v,) = take(1)
-    side_v, beside_v, picked_v, picked_parent_v, table_v = take(5)
+    side_v, beside_v, picked_v, picked_parent_v, table_v, target_near_v = take(6)
     load_sem, near_send, near_recv, tree_send, block_recv, id_send, id_recv = take(7)
 
     group, tile = (lax.axis_index("rhombus"), lax.axis_index("tile"))
@@ -100,8 +101,10 @@
     if pairs == 4:
         beside = pair + 1 - 2 * (pair % 2)
         level = [beside, (pair + 2) % 4, (beside + 2) % 4]
+        around = BY_HEIGHT if groups == 4 else ()
     else:
         level = [(pair + k) % pairs for k in range(1, pairs)]
+        around = ()
     row_peers = [at(group, other, core) for other in level]
     partner = at(group, pair, 1 - core)
     peers = columns + row_peers + [partner]
@@ -143,9 +146,7 @@
             load("edges", *ids, whole=edge_ids_v)
         if n == 4:
             load("coarse", (coarse_ref, coarse_v))
-    load("node_w1", (weight_refs["node_w1"], held["node_w1"]))
-    rest = FINISH_WEIGHTS[1:]
-    load("handed", *[(weight_refs[name], held[name]) for name in rest], whole=handed_v.at[pl.ds(1, len(rest))])
+    load("handed", *[(weight_refs[name], held[name]) for name in FINISH_WEIGHTS], whole=handed_v)
     waited = set()
 
     def await_load(name):
@@ -154,11 +155,8 @@
             waited.add(name)
 
     def weight(name):
-        if name == "node_w1":
-            await_load(name)
-        else:
-            place = GATHER_WEIGHTS.index(name)
-            await_load(next(n for n in range(len(LOADS)) if place < sum(LOADS[: n + 1])))
+        place = GATHER_WEIGHTS.index(name)
+        await_load(next(n for n in range(len(LOADS)) if place < sum(LOADS[: n + 1])))
         return held[name][...]
 
     me = group * tiles + tile
@@ -280,6 +278,41 @@
     table_v[:features, fines + 2 * rims :] = flipped(flip_v[1], fine_v[...]).astype(bf16)
     flip_v[0] = jnp.transpose(weight("edge_w_src"))
     table_v[:features, :fines] = flipped(flip_v[0], fine_v[...]).astype(bf16)
+    own_near = (1 + shift) * mids + within
+    step = next(size for size in (512, 256, 128) if edges % size == 0)
+    sources = fines + 2 * rims
+    line = lax.broadcasted_iota(i32, (table_v.shape[0] - features, fines), 0)
+    table_v[features:, sources:] = jnp.where(line == 1, own_near, 0).astype(f32).astype(bf16)
+
+    def known_target(i):
+        span = pl.ds(i * step, step)
+        target_pick = one_hot(edge_ids_v[1, :, span], 0, (fines, step))
+        target_v[:, span] = target_pick
+        found = product(table_v[:, sources:], target_pick)
+        known_v[:, span] = found[:features].astype(bf16)
+        target_near_v[:, span] = found[features + 1 : features + 2].astype(i32)
+
+    def known(i):
+        span = pl.ds(i * step, step)
+        source_pick = one_hot(edge_ids_v[0, :, span], 0, (sources, step))
+        if i < EARLY:
+            found = product(table_v[:, :sources], source_pick)
+            known_v[:, span] = (found[:features] + known_v[:, span].astype(f32)).astype(bf16)
+            target_near = target_near_v[:, span]
+        else:
+            target_pick = one_hot(edge_ids_v[1, :, span], 0, (fines, step))
+            target_v[:, span] = target_pick
+            found = product(table_v[...], jnp.concatenate([source_pick, target_pick], axis=0))
+            known_v[:, span] = found[:features].astype(bf16)
+            target_near = found[features + 1 : features + 2].astype(i32)
+        source_near = found[features : features + 1].astype(i32)
+        line = lax.broadcasted_iota(i32, (8 * mids, step), 0)
+        hit = (line == source_near) | (line == target_near + 5 * mids)
+        lookup_v[:, span] = jnp.where(hit, 1.0, 0.0).astype(bf16)
+
+    await_load("edges")
+    for i in range(EARLY):
+        known_target(i)
     mid_w3 = weight("mid_w3")
 
     @pl.when(tile > 0)
@@ -331,7 +364,7 @@
         return n if groups == 4 else order.index((groups - order[n]) % groups)
 
     def spread(n):
-        send(pair, n, row_peers, groups + n)
+        send(pair, n, row_peers[:-1] if n in around else row_peers, groups + n)
         send(pair, n, [partner], 2 * groups + n)
 
     for n in range(1, groups):
@@ -346,14 +379,6 @@
 
     def keep_message():
         message_v[...] = product(weight("w_coarse"), weight("coarse_w2")).astype(bf16)
-
-    def keep_ending():
-        ending_v[...] = product(weight("edge_w2"), weight("node_w2")).astype(bf16)
-
-    def keep_first():
-        first_v[...] = product(fine_v[...], weight("node_w1"))
-
-    own_near = (1 + shift) * mids + within
 
     def fill_table():
         @pl.when(tile > 0)
@@ -369,37 +394,19 @@
         table_v[:features, fines : fines + 2 * rims] = flipped(flip_v[0], rim_ref[...]).astype(bf16)
         far = jnp.concatenate([rim_parent_ref[0], rim_parent_ref[1]], axis=1)
         far = jnp.where(far < 0, -1, far - (me - 2) * mids)
-        blank = jnp.zeros((1, fines), i32)
-        source_parent = jnp.concatenate([own_near + mids, far, blank], axis=1)
-        target_parent = jnp.concatenate([blank, jnp.zeros((1, 2 * rims), i32), own_near], axis=1)
-        line = lax.broadcasted_iota(i32, (table_v.shape[0] - features, table_v.shape[1]), 0)
-        named = jnp.where(line == 0, source_parent, jnp.where(line == 1, target_parent, 0))
-        table_v[features:] = named.astype(f32).astype(bf16)
+        source_parent = jnp.concatenate([own_near + mids, far], axis=1)
+        line = lax.broadcasted_iota(i32, (table_v.shape[0] - features, sources), 0)
+        table_v[features:, :sources] = jnp.where(line == 0, source_parent, 0).astype(f32).astype(bf16)
         lift_v[...] = one_hot(as_columns(own_near, lift_v.shape[1]), 1, lift_v.shape)
 
-    step = next(size for size in (512, 256, 128) if edges % size == 0)
-
-    def known(i):
-        span = pl.ds(i * step, step)
-        source_pick = one_hot(edge_ids_v[0, :, span], 0, (fines + 2 * rims, step))
-        target_pick = one_hot(edge_ids_v[1, :, span], 0, (fines, step))
-        target_v[:, span] = target_pick
-        found = product(table_v[...], jnp.concatenate([source_pick, target_pick], axis=0))
-        known_v[:, span] = found[:features].astype(bf16)
-        source_near = found[features : features + 1].astype(i32)
-        target_near = found[features + 1 : features + 2].astype(i32) + 5 * mids
-        line = lax.broadcasted_iota(i32, (8 * mids, step), 0)
-        lookup_v[:, span] = jnp.where((line == source_near) | (line == target_near), 1.0, 0.0).astype(bf16)
-
     blocks_of_edges = iter(range(edges // step))
 
     def do_known(n=1):
-        await_load("edges")
         for i in [i for _, i in zip(range(n), blocks_of_edges)]:
             known(i)
 
-    def coarse_part(ns, cores):
-        places = [(heights[n], c) for c in cores for n in ns]
+    def coarse_part(pieces):
+        places = [(heights[n], c) for n, c in pieces]
         blocks = [ups_ref[pl.ds(place_of(h, 0, c), pairs)].reshape(pairs * mids, features) for h, c in places]
         slots = [id_place_of(h, p, c) for h, c in places for p in range(pairs)]
         id_row = jnp.concatenate([ids_ref[slot][:, :mids] for slot in slots], axis=1)
@@ -426,7 +433,14 @@
         spread(n)
 
     def across_at(n):
-        arrive(0, len(level), groups + n)
+        if n in around:
+            arrive(0, len(level) - 1, groups + n)
+            arrive(0, 1, 3 * groups + n)
+        else:
+            arrive(0, len(level), groups + n)
+        if n == 0:
+            for m in around:
+                send(level[-1], 0, [columns[m - 1]], 3 * groups + m)
         for other in level:
             send(other, n, [partner], 2 * groups + n)
 
@@ -443,32 +457,25 @@
     keep_message()
     ids_across()
     fill_table()
-    do_known()
+    do_known(1)
+    keep_coarse()
     relay(columns_left, column_at)
-    do_known()
+    do_known(1)
     relay(columns_left, column_at)
-    keep_coarse()
+    relay(across_left, across_at)
     relay(columns_left, column_at, groups)
-    do_known()
+    ids_partner()
+    do_known(3)
     relay(across_left, across_at)
-    ids_partner()
-    do_known()
-    keep_ending()
-    keep_first()
-    relay(across_left, across_at)
-    do_known()
     relay(across_left, across_at)
     ids_done()
     find_near()
-    early = range(groups - 1)
-    gained_v[...] = coarse_part(early, [core])
+    gained_v[...] = coarse_part([(n, core) for n in range(groups - 1)])
     relay(across_left, across_at, groups)
     do_known(edges)
-    for n in early:
+    for n in range(groups):
         partner_at(n)
-    gained_v[...] += coarse_part(early, [1 - core])
-    partner_at(groups - 1)
-    gained_v[...] += coarse_part([groups - 1], [core, 1 - core])
+    gained_v[...] += coarse_part([(groups - 1, core)] + [(n, 1 - core) for n in range(groups)])
     near_v[...] = jnp.concatenate([ups_ref[place_of(*place)] for place in nearby], axis=0)
 
     @pl.when(tile > 0)
@@ -492,10 +499,10 @@
 
 
 def finish_kernel(*refs):
-    pre_v, known_v, lookup_v, target_v, first_v, fine_v, coarse_v = refs[:7]
-    near_v, pick_v, lift_v, flip_v, ending_v, handed_v, message_v, gained_v = refs[7:15]
-    fine_out_ref, mid_out_ref, coarse_out_ref = refs[15:18]
-    fine_out_v, mid_out_v, coarse_out_v, padded_v, sums_v, out_sem = refs[18:]
+    pre_v, known_v, lookup_v, target_v, fine_v, coarse_v = refs[:6]
+    near_v, pick_v, lift_v, flip_v, handed_v, message_v, gained_v = refs[6:13]
+    fine_out_ref, mid_out_ref, coarse_out_ref = refs[13:16]
+    fine_out_v, mid_out_v, coarse_out_v, padded_v, sums_v, first_v, ending_v, out_sem = refs[16:]
     window, padded = pick_v.shape
     mids = mid_out_v.shape[0]
     fines, features = fine_v.shape
@@ -508,8 +515,24 @@
         outs.append(pltpu.make_async_copy(source, target, out_sem.at[len(outs)]))
         outs[-1].start()
 
-    hidden = gate(pre_v[...] + product(gained_v[...].astype(bf16), message_v[...])).astype(bf16)
-    updated = (coarse_v[...].astype(f32) + normed(product(hidden, weights["coarse_w3"][...]))).astype(bf16)
+    quarter = features // 4
+    fills = iter(range(8))
+
+    def fill(n=1):
+        for i in [i for _, i in zip(range(n), fills)]:
+            part = slice(i % 4 * quarter, (i % 4 + 1) * quarter)
+            if i < 4:
+                ending_v[part] = product(weights["edge_w2"][part], weights["node_w2"][...]).astype(bf16)
+            else:
+                rows = slice(i % 4 * fines // 4, (i % 4 + 1) * fines // 4)
+                first_v[rows] = product(fine_v[rows], weights["node_w1"][...])
+
+    message = product(gained_v[...].astype(bf16), message_v[...])
+    fill(2)
+    hidden = gate(pre_v[...] + message).astype(bf16)
+    change_out = product(hidden, weights["coarse_w3"][...])
+    fill(2)
+    updated = (coarse_v[...].astype(f32) + normed(change_out)).astype(bf16)
     coarse_out_v[...] = updated
     put(coarse_out_v, coarse_out_ref)
     edge = coarse_count // 16 * 16
@@ -517,11 +540,14 @@
     padded_v[:coarse_count] = updated
 
     picked = product(pick_v[...], padded_v[...]).astype(bf16)
+    fill()
     down = product(picked, weights["w_descend"][...])
+    fill()
     near_out = (near_v[...].astype(f32) + down).astype(bf16)
     mid_out_v[...] = near_out[2 * mids : 3 * mids]
     put(mid_out_v, mid_out_ref)
     fine_down = product(near_out, weights["w_fine"][...]).astype(bf16)
+    fill(8)
     beside = fine_down[mids : 4 * mids]
 
     def blank(rows):
@@ -532,6 +558,14 @@
     change = (flipped(flip_v[0], source_rows) + flipped(flip_v[1], target_rows)).astype(bf16)
 
     step = next(size for size in (1024, 512, 256, 128) if edges % size == 0)
+    spare = lift_v.shape[1] - 3 * mids
+    beside_first = product(beside, weights["node_w1"][...]).astype(bf16)
+    lift = lift_v[...]
+    if spare:
+        beside = jnp.concatenate([beside, blank(spare)], axis=0)
+        beside_first = jnp.concatenate([beside_first, blank(spare)], axis=0)
+    lifted = (fine_v[...].astype(f32) + product(lift, beside)).astype(bf16)
+    incoming = first_v[...] + product(lift, beside_first)
     total = None
     for i in range(edges // step):
         span = slice(i * step, (i + 1) * step)
@@ -542,19 +576,11 @@
         else:
             sums_v[...] += part
 
-    spare = lift_v.shape[1] - 3 * mids
-    beside_first = product(beside, weights["node_w1"][...]).astype(bf16)
-    lift = lift_v[...]
-    if spare:
-        beside = jnp.concatenate([beside, blank(spare)], axis=0)
-        beside_first = jnp.concatenate([beside_first, blank(spare)], axis=0)
-    lifted = (fine_v[...].astype(f32) + product(lift, beside)).astype(bf16)
-    incoming = first_v[...] + product(lift, beside_first)
     incoming += product(sums_v[...].astype(bf16), ending_v[...])
     hidden = gate(incoming).astype(bf16)
     rows = fines // 2
-    for half in range(2):
-        span = slice(half * rows, (half + 1) * rows)
+    for part in range(2):
+        span = slice(part * rows, (part + 1) * rows)
         result = lifted[span].astype(f32) + normed(product(hidden[span], weights["node_w3"][...]))
         fine_out_v[span] = result.astype(bf16)
         put(fine_out_v.at[span], fine_out_ref.at[span])
@@ -628,14 +654,12 @@
         pltpu.VMEM((features, edges), bf16),
         pltpu.VMEM((8 * mids, edges), bf16),
         pltpu.VMEM((fines, edges), bf16),
-        pltpu.VMEM((fines, features), f32),
         pltpu.VMEM((fines, features), bf16),
         pltpu.VMEM((coarse_count, features), bf16),
         pltpu.VMEM((5 * mids, features), bf16),
         pltpu.VMEM((5 * mids, ceil(coarse_count)), bf16),
         pltpu.VMEM((fines, ceil(3 * mids)), bf16),
         pltpu.VMEM((2, *square), bf16),
-        pltpu.VMEM(square, bf16),
         pltpu.VMEM((len(FINISH_WEIGHTS), *square), bf16),
         pltpu.VMEM(square, bf16),
         pltpu.VMEM((coarse_count, features), f32),
@@ -658,11 +682,12 @@
             pltpu.VMEM((halos, features), bf16),
             pltpu.VMEM((2, 1, rims), i32),
             pltpu.VMEM((features + 16, 2 * fines + halos), bf16),
-            dma((len(small) + 5 + len(LOADS),)),
+            pltpu.VMEM((1, edges), i32),
+            dma((len(small) + 4 + len(LOADS),)),
             dma((6,)),
             dma((6,)),
             dma((1,)),
-            dma((3 * groups,)),
+            dma((4 * groups,)),
             dma((1,)),
             dma((pairs + 1,)),
         ],
@@ -684,7 +709,9 @@
             pltpu.VMEM((coarse_count, features), bf16),
             pltpu.VMEM((ceil(coarse_count), features), bf16),
             pltpu.VMEM((fines, features), f32),
-            dma((4,)),
+            pltpu.VMEM((fines, features), f32),
+            pltpu.VMEM(square, bf16),
+            dma((6,)),
         ],
         compiler_params=pltpu.CompilerParams(vmem_limit_bytes=24 << 20),
         name="sweep_finish",

time: 28.6 us -> 27.4 us (0.958)
  Pallas kernels: 27.8 us -> 26.6 us
    pallas_call x1, Pallas kernels: 20.5 us -> 19.7 us  [on_device(): pl.pallas_call(lambda *refs: gather_kernel(groups, tiles, *refs), out_sha...]
    pallas_call x1, Pallas kernels: 7.25 us -> 6.89 us  [on_device(): pl.pallas_call(finish_kernel, out_shape=(jax.ShapeDtypeStruct((fines, fea...]
where the time goes in v4:
time: 27.4 us; the launch traced here: 27.3 us
  Pallas kernels  26.6 us (97%)
  between operations  0.65 us (2%)
    pallas_call x1, Pallas kernels, on_device(): pl.pallas_call(lambda *refs: gather_kernel(groups, tiles, *refs), out_sha...  19.7 us
    pallas_call x1, Pallas kernels, on_device(): pl.pallas_call(finish_kernel, out_shape=(jax.ShapeDtypeStruct((fines, fea...  6.89 us

profile of v4, /device:TPU:0, one launch (start us, length us, event | category | flops | bytes accessed | tf_op | source)
XLA Modules:
  0.0 27.3 jit_solution(13029403108438399136)
XLA Ops:
  0.6 19.7 %sweep_gather.1 = (f32[642,512]{1,0:T(8,128)S(1)}, bf16[512,3072]{1,0:T(8,128)(2,1)S(1)}, bf16[256,3072]{1,0:T(8,128)(2,1)S(1)}, bf16[512,3072]{1,0:T(8,128)(2,1...) custom-call(s32[1,512]{1,0:T(1,128)} %bitcast.7, ...), custom_call_target="tpu_custom_call" | custom-call | tf_op jit(solution)/shard_map/sweep_gather/pallas_call | solution.py:667
  20.4 6.9 %sweep_finish.1 = (bf16[512,512]{1,0:T(8,128)(2,1)}, bf16[32,512]{1,0:T(8,128)(2,1)}, bf16[642,512]{1,0:T(8,128)(2,1)}) custom-call(f32[642,512]{1,0:T(8,128)S(1)} %get-tuple-element.16.refs_0_, bf16[512,3072]{1,0:T(8,128)(2,1)S(1)} %get-tuple-element.17.refs_1_, bf16[256,3072]{1,0:T(8,128)(2,1)S(1)} %get-tuple-element.18.refs_2_, ...), custom_call_target="tpu_custom_call" | custom-call | tf_op jit(solution)/shard_map/sweep_finish/pallas_call | solution.py:697

commit v5 on v4

--- a/solution.py
+++ b/solution.py
@@ -58,7 +58,7 @@
 )
 FINISH_WEIGHTS = ("coarse_w3", "edge_w2", "node_w2", "w_descend", "w_fine", "node_w1", "node_w3")
 EARLY = 0
-BY_HEIGHT = (1, 2)
+BY_HEIGHT = (1, 2, 3)
 SMALL = ("parent", "halo", "coarse_id", "latent")
 LOADS = (2, 2, 1, 1, 2, 1)
 
@@ -433,16 +433,17 @@
         spread(n)
 
     def across_at(n):
-        if n in around:
-            arrive(0, len(level) - 1, groups + n)
-            arrive(0, 1, 3 * groups + n)
-        else:
-            arrive(0, len(level), groups + n)
+        here = level[:-1] if n in around else level
+        arrive(0, len(here), groups + n)
         if n == 0:
             for m in around:
                 send(level[-1], 0, [columns[m - 1]], 3 * groups + m)
-        for other in level:
+        for other in here:
             send(other, n, [partner], 2 * groups + n)
+
+    def corner_at(n):
+        arrive(0, 1, 3 * groups + n)
+        send(level[-1], n, [partner], 2 * groups + n)
 
     def partner_at(n):
         arrive(place_of(heights[n], 0, 1 - core), pairs, 2 * groups + n)
@@ -457,21 +458,24 @@
     keep_message()
     ids_across()
     fill_table()
-    do_known(1)
+    do_known(2)
+    relay(columns_left, column_at)
     keep_coarse()
-    relay(columns_left, column_at)
-    do_known(1)
     relay(columns_left, column_at)
     relay(across_left, across_at)
     relay(columns_left, column_at, groups)
     ids_partner()
     do_known(3)
     relay(across_left, across_at)
-    relay(across_left, across_at)
+    relay(across_left, across_at, groups - 3)
+    for n in around[:-1]:
+        corner_at(n)
     ids_done()
     find_near()
     gained_v[...] = coarse_part([(n, core) for n in range(groups - 1)])
     relay(across_left, across_at, groups)
+    for n in around[-1:]:
+        corner_at(n)
     do_known(edges)
     for n in range(groups):
         partner_at(n)
@@ -578,9 +582,8 @@
 
     incoming += product(sums_v[...].astype(bf16), ending_v[...])
     hidden = gate(incoming).astype(bf16)
-    rows = fines // 2
-    for part in range(2):
-        span = slice(part * rows, (part + 1) * rows)
+    cut = fines - ceil(fines // 4, 16)
+    for span in (slice(0, cut), slice(cut, fines)):
         result = lifted[span].astype(f32) + normed(product(hidden[span], weights["node_w3"][...]))
         fine_out_v[span] = result.astype(bf16)
         put(fine_out_v.at[span], fine_out_ref.at[span])

time: 27.4 us -> 27 us (0.985)
  Pallas kernels: 26.6 us -> 26.2 us
    pallas_call x1, Pallas kernels: 19.7 us -> 19.4 us  [on_device(): pl.pallas_call(lambda *refs: gather_kernel(groups, tiles, *refs), out_sha...]
where the time goes in v5:
time: 27 us; the launch traced here: 26.9 us
  Pallas kernels  26.2 us (97%)
  between operations  0.65 us (2%)
    pallas_call x1, Pallas kernels, on_device(): pl.pallas_call(lambda *refs: gather_kernel(groups, tiles, *refs), out_sha...  19.4 us
    pallas_call x1, Pallas kernels, on_device(): pl.pallas_call(finish_kernel, out_shape=(jax.ShapeDtypeStruct((fines, fea...  6.82 us

profile of v5, /device:TPU:0, one launch (start us, length us, event | category | flops | bytes accessed | tf_op | source)
XLA Modules:
  0.0 26.9 jit_solution(5292929826366050257)
XLA Ops:
  0.6 19.4 %sweep_gather.1 = (f32[642,512]{1,0:T(8,128)S(1)}, bf16[512,3072]{1,0:T(8,128)(2,1)S(1)}, bf16[256,3072]{1,0:T(8,128)(2,1)S(1)}, bf16[512,3072]{1,0:T(8,128)(2,1...) custom-call(s32[1,512]{1,0:T(1,128)} %bitcast.7, ...), custom_call_target="tpu_custom_call" | custom-call | tf_op jit(solution)/shard_map/sweep_gather/pallas_call | solution.py:670
  20.0 6.8 %sweep_finish.1 = (bf16[512,512]{1,0:T(8,128)(2,1)}, bf16[32,512]{1,0:T(8,128)(2,1)}, bf16[642,512]{1,0:T(8,128)(2,1)}) custom-call(f32[642,512]{1,0:T(8,128)S(1)} %get-tuple-element.16.refs_0_, bf16[512,3072]{1,0:T(8,128)(2,1)S(1)} %get-tuple-element.17.refs_1_, bf16[256,3072]{1,0:T(8,128)(2,1)S(1)} %get-tuple-element.18.refs_2_, ...), custom_call_target="tpu_custom_call" | custom-call | tf_op jit(solution)/shard_map/sweep_finish/pallas_call | solution.py:700

commit v6 on v5

--- a/solution.py
+++ b/solution.py
@@ -364,7 +364,7 @@
         return n if groups == 4 else order.index((groups - order[n]) % groups)
 
     def spread(n):
-        send(pair, n, row_peers[:-1] if n in around else row_peers, groups + n)
+        send(pair, n, row_peers[:-1] if n in around else row_peers[::-1], groups + n)
         send(pair, n, [partner], 2 * groups + n)
 
     for n in range(1, groups):

time: 27 us -> 27 us (level)
  no operation moved by 1% of the time
where the time goes in v6:
time: 27 us; the launch traced here: 26.8 us
  Pallas kernels  26.2 us (97%)
  between operations  0.65 us (2%)
    pallas_call x1, Pallas kernels, on_device(): pl.pallas_call(lambda *refs: gather_kernel(groups, tiles, *refs), out_sha...  19.4 us
    pallas_call x1, Pallas kernels, on_device(): pl.pallas_call(finish_kernel, out_shape=(jax.ShapeDtypeStruct((fines, fea...  6.82 us

profile of v6, /device:TPU:0, one launch (start us, length us, event | category | flops | bytes accessed | tf_op | source)
XLA Modules:
  0.0 26.8 jit_solution(17624116399746623058)
XLA Ops:
  0.6 19.4 %sweep_gather.1 = (f32[642,512]{1,0:T(8,128)S(1)}, bf16[512,3072]{1,0:T(8,128)(2,1)S(1)}, bf16[256,3072]{1,0:T(8,128)(2,1)S(1)}, bf16[512,3072]{1,0:T(8,128)(2,1...) custom-call(s32[1,512]{1,0:T(1,128)} %bitcast.7, ...), custom_call_target="tpu_custom_call" | custom-call | tf_op jit(solution)/shard_map/sweep_gather/pallas_call | solution.py:670
  20.0 6.8 %sweep_finish.1 = (bf16[512,512]{1,0:T(8,128)(2,1)}, bf16[32,512]{1,0:T(8,128)(2,1)}, bf16[642,512]{1,0:T(8,128)(2,1)}) custom-call(f32[642,512]{1,0:T(8,128)S(1)} %get-tuple-element.16.refs_0_, bf16[512,3072]{1,0:T(8,128)(2,1)S(1)} %get-tuple-element.17.refs_1_, bf16[256,3072]{1,0:T(8,128)(2,1)S(1)} %get-tuple-element.18.refs_2_, ...), custom_call_target="tpu_custom_call" | custom-call | tf_op jit(solution)/shard_map/sweep_finish/pallas_call | solution.py:700
